TPU v7x, 32 devices: a whole 2x2x4 slice. The times are simulated.
32 devices in a mesh: rep: 8 (over y, x, core), exp: 4 (over z).
Axes of the slice: x: 2, y: 2, z: 4, core: 2. Of those that a mesh axis runs over, the one named last changes fastest.
Arguments:
- x_rows: bfloat16 [8, 512, 2048], P('rep', 'exp'), may hold values from -8 to 8
- row_cot: bfloat16 [8, 512, 2048], P('rep', 'exp'), may hold values from -8 to 8
- gate_vals: float32 [8, 512], P('rep', 'exp'), may hold values from 0 to 1, as said below
- route_pos: int32 [8, 80, 4], P('rep', 'exp'), may hold values from 0 to 115, as said below
- weights: bfloat16 [4, 3, 2048, 384], P('exp'), may hold values from -0.125 to 0.125
- momentum: float32 [4, 3, 2048, 384], P('exp', None, 'rep'), may hold values from -6 to 6
Outputs:
- token_grad: bfloat16 [8, 80, 2048], P('rep', 'exp')
- momentum_new: float32 [4, 3, 2048, 384], P('exp', None, 'rep')
Inputs may be any that keep to these rules, and one draw needn't show every extreme that they name: `route_pos`: for each token of an owner, 4 positions e * 32 + c in ascending order, from 4 different experts e; from expert e an owner refers to slots c = 0 .. n - 1, each by exactly one token, where n is at most 20 and equals 20 for some expert of every owner; in every replica some owner uses all 20 slots of the last expert and some owner all of expert 0. `gate_vals`: row o * 32 + c of an expert in a replica belongs to owner o's slot c; its weight is zero exactly where no token of that owner refers to the slot, and positive elsewhere.
All inputs are finite; a program needn't handle non-finite values.
Results may differ from a plain program's by a relative error of at most 0.0064.
Values may be sent and summed in bfloat16 or wider, within the bound.
No kernel may reach another device: no remote copies, remote signals or barrier semaphores. Data moves between devices by JAX's collectives and lax.ppermute only.
A program may use at most 64 MiB of HBM per device.

v0:
```python
import functools

import jax
import jax.numpy as jnp
from jax import lax
from jax.experimental import pallas as pl
from jax.experimental.pallas import tpu as pltpu
from jax.sharding import PartitionSpec as P

tiny_eps = 1e-06
moment_decay = 0.9
HIGHEST = lax.Precision.HIGHEST
pack_flops = 10**11
bf16, f32 = jnp.bfloat16, jnp.float32
contract_rows = (((0,), (0,)), ((), ()))
contract_cols = (((1,), (1,)), ((), ()))


def swap(block, axis, mask):
    count = lax.axis_size(axis)
    return lax.ppermute(block, axis, [(i, i ^ mask) for i in range(count)])


def live_rows(block, owners, live):
    width = block.shape[-1]
    return block.reshape(owners, -1, width)[:, :live].reshape(owners * live, width)


def backward_parts(gate_pre, up_pre, hidden_grad):
    sigma_gate = jax.nn.sigmoid(gate_pre)
    activation = gate_pre * sigma_gate
    hidden = (activation * up_pre).astype(bf16)
    gate_grad = (hidden_grad * up_pre * sigma_gate * (1.0 + gate_pre * (1.0 - sigma_gate))).astype(
        bf16
    )
    up_grad = (hidden_grad * activation).astype(bf16)
    return gate_grad, up_grad, hidden


VMEM = pl.BlockSpec(memory_space=pltpu.VMEM)
HBM = pl.BlockSpec(memory_space=pltpu.HBM)


def in_hbm(array):
    return pltpu.with_memory_space_constraint(array, pltpu.HBM)


def kernel_params(mib):
    return pltpu.CompilerParams(vmem_limit_bytes=mib << 20)


def spread_rows(index, live, cap, owners):
    place = index
    for owner in range(1, owners):
        place = place + jnp.where(index >= owner * live, cap - live, 0)
    return place


def pack_kernel(sizes, x_hbm, cot_hbm, gate_hbm, *refs):
    owners, cap, live, chips, width, _ = sizes
    out_refs, (x_ref, cot_ref, gate_ref, sems, gate_sem) = refs[:chips], refs[chips:]
    slots, rows = owners * cap, owners * live
    chip = lax.axis_index("rep") >> 1
    gate_copy = pltpu.make_async_copy(gate_hbm, gate_ref, gate_sem)
    gate_copy.start()
    copies = []
    for k in range(chips):
        at = pl.ds(pl.multiple_of((chip ^ k) * 2 * width, 2 * width), 2 * width)
        for side, (source, target) in enumerate([(x_hbm, x_ref), (cot_hbm, cot_ref)]):
            copy = pltpu.make_async_copy(source.at[0, :, at], target.at[k], sems.at[k, side])
            copy.start()
            copies.append(copy)
    place = spread_rows(lax.broadcasted_iota(jnp.int32, (rows, slots), 0), live, cap, owners)
    slot = lax.broadcasted_iota(jnp.int32, (rows, slots), 1)
    select = jnp.where(place == slot, 1.0, 0.0).astype(bf16)
    line = lax.broadcasted_iota(jnp.int32, (slots, slots), 0)
    lane = lax.broadcasted_iota(jnp.int32, (slots, slots), 1)
    gate_copy.wait()
    gate = jnp.sum(jnp.where(line == lane, gate_ref[...], 0.0), axis=1, keepdims=True)
    for k in range(chips):
        copies[2 * k].wait()
        copies[2 * k + 1].wait()
        scaled = (gate * cot_ref[k].astype(f32)).astype(bf16)
        routed = jnp.dot(select, x_ref[k], preferred_element_type=f32).astype(bf16)
        scaled = jnp.dot(select, scaled, preferred_element_type=f32).astype(bf16)
        for core in range(2):
            out_refs[k][core, :, :width] = routed[:, core * width : (core + 1) * width]
            out_refs[k][core, :, width:] = scaled[:, core * width : (core + 1) * width]


def pack_call(x_rows, row_cot, gate_vals, sizes):
    owners, cap, live, chips, width, _ = sizes
    rows = owners * live
    return pl.pallas_call(
        functools.partial(pack_kernel, sizes),
        out_shape=[jax.ShapeDtypeStruct((2, rows, 2 * width), bf16)] * chips,
        in_specs=[HBM] * 3,
        out_specs=[VMEM] * chips,
        scratch_shapes=[
            pltpu.VMEM((chips, owners * cap, 2 * width), bf16),
            pltpu.VMEM((chips, owners * cap, 2 * width), bf16),
            pltpu.VMEM((1, owners * cap), f32),
            pltpu.SemaphoreType.DMA((chips, 2)),
            pltpu.SemaphoreType.DMA,
        ],
        compiler_params=kernel_params(6),
        cost_estimate=pl.CostEstimate(
            flops=pack_flops, bytes_accessed=8 * x_rows.size, transcendentals=0
        ),
        name="pack",
    )(in_hbm(x_rows), in_hbm(row_cot), in_hbm(gate_vals))


def forward_kernel(sizes, *refs):
    _, _, _, chips, width, ff = sizes
    pair_refs, w_ref, small_ref = refs[:chips], refs[chips], refs[chips + 1]
    chip = lax.axis_index("rep") >> 1
    sums = [None] * 3
    for k in range(chips):
        for core in range(2):
            at = pl.ds(pl.multiple_of(((chip ^ k) * 2 + core) * width, width), width)
            for t in range(3):
                left = pair_refs[k][core, :, width:] if t == 2 else pair_refs[k][core, :, :width]
                part = jnp.dot(left, w_ref[0, t, at, :], preferred_element_type=f32)
                sums[t] = part if sums[t] is None else sums[t] + part
    for t, part in enumerate(backward_parts(*sums)):
        small_ref[:, t * ff : (t + 1) * ff] = part


def forward_call(pairs, weights, sizes):
    owners, _, live, chips, _, ff = sizes
    rows = owners * live
    return pl.pallas_call(
        functools.partial(forward_kernel, sizes),
        out_shape=jax.ShapeDtypeStruct((rows, 3 * ff), bf16),
        in_specs=[VMEM] * (chips + 1),
        out_specs=VMEM,
        compiler_params=kernel_params(7),
        cost_estimate=pl.CostEstimate(
            flops=2 * rows * weights.size,
            bytes_accessed=2 * weights.size,
            transcendentals=rows * ff,
        ),
        name="forward",
    )(*pairs, weights)


def back_kernel(sizes, small_ref, w_ref, *out_refs):
    owners, cap, live, chips, width, ff = sizes
    slots, rows = owners * cap, owners * live
    me = lax.axis_index("exp")
    slot = lax.broadcasted_iota(jnp.int32, (slots, rows), 0)
    row = lax.broadcasted_iota(jnp.int32, (slots, rows), 1)
    place = jnp.full((slots, rows), -1, jnp.int32)
    for k in range(owners):
        inside = (slot >= k * cap) & (slot < k * cap + live)
        place = jnp.where(inside, slot - k * cap + (me ^ k) * live, place)
    select = jnp.where(place == row, 1.0, 0.0).astype(bf16)
    spread = jnp.dot(select, small_ref[:, : 2 * ff], preferred_element_type=f32).astype(bf16)
    chunk = 2 * width
    for c in range(chips):
        at = slice(c * chunk, (c + 1) * chunk)
        grad = lax.dot_general(
            spread[:, :ff], w_ref[0, 0, at, :], contract_cols, preferred_element_type=f32
        ) + lax.dot_general(
            spread[:, ff:], w_ref[0, 1, at, :], contract_cols, preferred_element_type=f32
        )
        grad = grad.astype(bf16)
        for k in range(owners):
            out_refs[k][:, at] = grad[k * cap : k * cap + live]


def back_call(small, weights, sizes):
    owners, _, live, _, _, ff = sizes
    rows, depth = owners * live, weights.shape[2]
    return pl.pallas_call(
        functools.partial(back_kernel, sizes),
        out_shape=[jax.ShapeDtypeStruct((live, depth), bf16)] * owners,
        in_specs=[VMEM] * 2,
        out_specs=[VMEM] * owners,
        compiler_params=kernel_params(7),
        cost_estimate=pl.CostEstimate(
            flops=4 * rows * depth * ff,
            bytes_accessed=weights.size * 4 // 3,
            transcendentals=0,
        ),
        name="back",
    )(small, weights)


def token_kernel(cap, route_ref, *refs):
    row_refs, out_ref, held = refs[:-2], refs[-2], refs[-1]
    owners, live = len(row_refs), row_refs[0].shape[0]
    me = lax.axis_index("exp")
    held[...] = jnp.zeros_like(held)
    for k in range(owners):
        held[k * cap : k * cap + live] = row_refs[k][...]
    picks, tokens = route_ref.shape[1:]
    line = lax.broadcasted_iota(jnp.int32, (owners * cap, tokens), 0)
    place = line
    for k in range(owners):
        inside = (line >= k * cap) & (line < (k + 1) * cap)
        place = jnp.where(inside, line + ((me ^ k) - k) * cap, place)
    choice = jnp.zeros((owners * cap, tokens), f32)
    for pick in range(picks):
        choice = choice + jnp.where(route_ref[0, pick : pick + 1, :] == place, 1.0, 0.0)
    sums = lax.dot_general(
        choice.astype(bf16), held[...], contract_rows, preferred_element_type=f32
    )
    out_ref[0] = sums.astype(bf16)


def token_call(route_pos, returned, cap):
    owners, (live, depth) = len(returned), returned[0].shape
    return pl.pallas_call(
        functools.partial(token_kernel, cap),
        out_shape=jax.ShapeDtypeStruct((1, route_pos.shape[1], depth), bf16),
        in_specs=[VMEM] * (owners + 1),
        out_specs=VMEM,
        scratch_shapes=[pltpu.VMEM((owners * cap, depth), bf16)],
        compiler_params=kernel_params(6),
        cost_estimate=pl.CostEstimate(
            flops=2 * route_pos.shape[1] * owners * cap * depth,
            bytes_accessed=owners * live * depth * 4,
            transcendentals=0,
        ),
        name="token",
    )(route_pos.swapaxes(1, 2), *returned)


def tall_kernel(reps, *refs):
    tall_refs, gram_ref, flip_ref = refs[:reps], refs[reps], refs[reps + 1]
    width = tall_refs[0].shape[2] // 2
    core = lax.axis_index("rep") & 1
    for side in range(2):
        at = slice(side * width, (side + 1) * width)
        both = jnp.concatenate(
            [jnp.concatenate([ref[0, :, at], ref[1, :, at]], axis=1) for ref in tall_refs], axis=0
        )
        gram_ref[side] = lax.dot_general(both, both, contract_cols, preferred_element_type=f32)
        own = jnp.concatenate([ref[core, :, at] for ref in tall_refs], axis=0)
        flip_ref[side] = own.T


def tall_call(tall):
    reps, (cores, rows, width) = len(tall), tall[0].shape
    width //= 2
    flat = reps * rows
    return pl.pallas_call(
        functools.partial(tall_kernel, reps),
        out_shape=[
            jax.ShapeDtypeStruct((2, flat, flat), f32),
            jax.ShapeDtypeStruct((2, width, flat), bf16),
        ],
        in_specs=[VMEM] * reps,
        out_specs=[VMEM] * 2,
        compiler_params=kernel_params(6),
        cost_estimate=pl.CostEstimate(
            flops=8 * flat * flat * width,
            bytes_accessed=8 * flat * flat + 12 * flat * width,
            transcendentals=0,
        ),
        name="tall",
    )(*tall)


def gram_kernel(reps, ff, *refs):
    wide_refs, tall_ref, out_ref = refs[:reps], refs[reps], refs[reps + 1]
    rows = wide_refs[0].shape[0]
    flat = reps * rows
    me = lax.axis_index("rep")
    spot = lax.broadcasted_iota(jnp.int32, (flat, 128), 0)
    lane = lax.broadcasted_iota(jnp.int32, (flat, 128), 1)
    group = jnp.zeros_like(spot)
    for k in range(1, reps):
        group = group + jnp.where(spot >= k * rows, 1, 0)
    gather = jnp.where((group ^ me) == (lane & (reps - 1)), 1.0, 0.0)
    sums = []
    for t in range(3):
        block = jnp.concatenate([ref[:, t * ff : (t + 1) * ff] for ref in wide_refs], axis=0)
        both = lax.dot_general(block, block, contract_cols, preferred_element_type=f32)
        both = both * tall_ref[t // 2]
        sums.append(jnp.sum(both.reshape(reps, rows // 8, 8, flat), axis=1).reshape(reps * 8, flat))
    sums = jnp.dot(
        jnp.concatenate(sums, axis=0), gather, precision=HIGHEST, preferred_element_type=f32
    )
    sums = jnp.sum(sums.reshape(3 * reps, 8, 128), axis=1)
    for t in range(3):
        for k in range(reps):
            out_ref[pl.ds(t * reps + (me ^ k), 1), :] = sums[t * reps + k : t * reps + k + 1]


def gram_call(wide, tall_gram, ff):
    reps, rows = len(wide), wide[0].shape[0]
    flat = reps * rows
    return pl.pallas_call(
        functools.partial(gram_kernel, reps, ff),
        out_shape=jax.ShapeDtypeStruct((3 * reps, 128), f32),
        in_specs=[VMEM] * (reps + 1),
        out_specs=VMEM,
        compiler_params=kernel_params(6),
        cost_estimate=pl.CostEstimate(
            flops=6 * flat * flat * ff,
            bytes_accessed=8 * flat * flat + 6 * flat * ff,
            transcendentals=0,
        ),
        name="gram",
    )(*wide, tall_gram)


def final_kernel(reps, ff, gram_ref, other_ref, flip_ref, *refs):
    wide_refs, moment_ref, out_ref, coef_ref = refs[:reps], refs[reps], refs[reps + 1], refs[reps + 2]
    me = lax.axis_index("rep")
    line = lax.broadcasted_iota(jnp.int32, (reps, 128), 0)
    lane = lax.broadcasted_iota(jnp.int32, (reps, 128), 1)
    near = lane & (reps - 1)
    for t in range(3):
        part = slice(t * reps, (t + 1) * reps)
        gram = gram_ref[part, :] + other_ref[part, :]
        coefs = jnp.ones((reps, 128), f32)
        half = reps // 2
        while half >= 1:

            def factor(axis, spot):
                square = jnp.where(spot == line, gram, 0.0)
                square = jnp.maximum(jnp.sum(square, axis=axis, keepdims=True), 0.0)
                square = jnp.broadcast_to(square, (reps, 128))
                inner = jnp.where(spot == line ^ half, gram, 0.0)
                inner = jnp.sum(inner, axis=axis, keepdims=True)
                bound = jnp.sqrt(square * pltpu.roll(square, half, 1 - axis))
                inner = jnp.clip(inner, -bound, bound)
                return 1.0 - inner / (2.0 * (square + tiny_eps))

            by_line, by_lane = factor(1, lane), factor(0, near)
            coefs = coefs * by_line
            gram = gram * by_line * by_lane
            gram = gram + pltpu.roll(gram, half, 0)
            gram = gram + pltpu.roll(gram, half, 1)
            half //= 2
        coef_ref[part, :] = jnp.concatenate([coefs] * (ff // 128), axis=1)
    for t in range(3):
        scaled = []
        for k in range(reps):
            coef = coef_ref[pl.ds(t * reps + (me ^ k), 1), :]
            scaled.append((coef * wide_refs[k][:, t * ff : (t + 1) * ff].astype(f32)).astype(bf16))
        combined = jnp.dot(
            flip_ref[t // 2], jnp.concatenate(scaled, axis=0), preferred_element_type=f32
        )
        out_ref[0, t] = moment_decay * moment_ref[0, t] + (1.0 - moment_decay) * combined


def final_call(gram, other, flip, wide, momentum, ff):
    reps, rows = len(wide), wide[0].shape[0]
    return pl.pallas_call(
        functools.partial(final_kernel, reps, ff),
        out_shape=jax.ShapeDtypeStruct(momentum.shape, f32),
        in_specs=[VMEM] * (reps + 4),
        out_specs=VMEM,
        scratch_shapes=[pltpu.VMEM((3 * reps, ff), f32)],
        compiler_params=kernel_params(6),
        cost_estimate=pl.CostEstimate(
            flops=2 * reps * rows * momentum.size,
            bytes_accessed=8 * momentum.size + 6 * reps * rows * ff,
            transcendentals=0,
        ),
        name="final",
    )(gram, other, flip, *wide, momentum)


def adasum_weights(gram):
    count = gram.shape[-1]
    index = jnp.arange(count)
    weights = jnp.ones(gram.shape[:2], f32)
    half = count // 2
    while half >= 1:
        partner = index ^ half
        square = jnp.maximum(jnp.sum(jnp.where(index[:, None] == index[None, :], gram, 0.0), 2), 0.0)
        inner = jnp.sum(jnp.where(partner[:, None] == index[None, :], gram, 0.0), 2)
        bound = jnp.sqrt(square * square[:, partner])
        inner = jnp.clip(inner, -bound, bound)
        coef = 1.0 - inner / (2.0 * (square + tiny_eps))
        weights = weights * coef
        gram = gram * coef[:, :, None] * coef[:, None, :]
        gram = gram + gram[:, partner]
        gram = gram + gram[:, :, partner]
        half //= 2
    return weights


def forward_plain(x_rows, row_cot, gate_vals, weights, sizes):
    owners, _, live, chips, width, _ = sizes
    routed = live_rows(x_rows[0], owners, live)
    out_cot = live_rows(row_cot[0], owners, live)
    gate_row = live_rows(gate_vals[0][:, None], owners, live)
    rows = routed.shape[0]
    scaled = (gate_row * out_cot.astype(f32)).astype(bf16)
    gate_pre = jnp.dot(routed, weights[0, 0], preferred_element_type=f32)
    up_pre = jnp.dot(routed, weights[0, 1], preferred_element_type=f32)
    hidden_grad = jnp.dot(scaled, weights[0, 2], preferred_element_type=f32)
    small = jnp.concatenate(backward_parts(gate_pre, up_pre, hidden_grad), axis=1)
    sides = [routed.reshape(rows, 2 * chips, width), scaled.reshape(rows, 2 * chips, width)]
    slices = jnp.concatenate(sides, axis=2).transpose(1, 0, 2)
    return slices, small


def gram_plain(lefts, rights):
    grams = []
    for left, right in zip(lefts, rights, strict=True):
        each = jnp.einsum("rnd,rnf->rdf", left, right, preferred_element_type=f32)
        grams.append(jnp.einsum("rdf,sdf->rs", each, each, precision=HIGHEST))
    return jnp.stack(grams)


def final_plain(coefs, lefts, rights, momentum):
    combined = []
    for t in range(3):
        right = (coefs[t][:, None, None] * rights[t].astype(f32)).astype(bf16)
        left = lefts[t].reshape(-1, lefts[t].shape[2])
        combined.append(
            lax.dot_general(
                left, right.reshape(-1, right.shape[2]), contract_rows, preferred_element_type=f32
            )
        )
    return moment_decay * momentum + (1.0 - moment_decay) * jnp.stack(combined)[None]


def back_plain(small, weights, sizes):
    owners, live, ff = sizes[0], sizes[2], sizes[5]
    grad = lax.dot_general(small[:, :ff], weights[0, 0], contract_cols, preferred_element_type=f32)
    grad = grad + lax.dot_general(
        small[:, ff : 2 * ff], weights[0, 1], contract_cols, preferred_element_type=f32
    )
    return grad.astype(bf16).reshape(owners, live, -1)


def token_plain(route_pos, returned, cap):
    owners, live, depth = returned.shape
    place = route_pos[0] // cap * live + route_pos[0] % cap
    picks = jnp.sum(place[:, :, None] == jnp.arange(owners * live)[None, None, :], axis=1)
    returned = returned.reshape(owners * live, depth)
    return jnp.dot(picks.astype(bf16), returned, preferred_element_type=f32).astype(bf16)[None]


def all_swaps(blocks, axis, scale):
    got = []
    for k, block in enumerate(blocks):
        got.append(swap(block, axis, k * scale) if k else block)
    return got


def core_swaps(blocks):
    got = []
    for mine in blocks:
        got += [mine, swap(mine, "rep", 1)]
    return got


def with_kernels(x_rows, row_cot, gate_vals, route_pos, weights, momentum, sizes):
    _, cap, _, chips, _, ff = sizes
    pairs = pack_call(x_rows, row_cot, gate_vals, sizes)
    tall = all_swaps(pairs, "rep", 2)
    small = forward_call(pairs, weights, sizes)
    wide = all_swaps([small] * chips, "rep", 2)
    returned = all_swaps(back_call(small, weights, sizes), "exp", 1)
    token_grad = token_call(route_pos, returned, cap)
    tall, wide = core_swaps(tall), core_swaps(wide)
    tall_gram, flip = tall_call(tall)
    gram = gram_call(wide, tall_gram, ff)
    mask = chips
    while mask > 2:
        gram = gram + swap(gram, "rep", mask)
        mask //= 2
    other = swap(gram, "rep", 2)
    return token_grad, final_call(gram, other, flip, wide, momentum, ff)


def without_kernels(x_rows, row_cot, gate_vals, route_pos, weights, momentum, sizes):
    _, cap, _, chips, width, ff = sizes
    reps = 2 * chips
    slices, small = forward_plain(x_rows, row_cot, gate_vals, weights, sizes)
    tall = lax.all_to_all(slices, "rep", split_axis=0, concat_axis=0, tiled=True)
    wide = jnp.stack(core_swaps(all_swaps([small] * chips, "rep", 2)))
    returned = back_plain(small, weights, sizes)
    returned = lax.all_to_all(returned, "exp", split_axis=0, concat_axis=0, tiled=True)
    token_grad = token_plain(route_pos, returned, cap)
    order = jnp.arange(reps) ^ lax.axis_index("rep")
    tall = tall[order]
    lefts = [tall[:, :, :width], tall[:, :, :width], tall[:, :, width:]]
    rights = [wide[:, :, t * ff : (t + 1) * ff] for t in range(3)]
    gram = gram_plain(lefts, rights)[:, order][:, :, order]
    mask = chips
    while mask >= 1:
        gram = gram + swap(gram, "rep", mask)
        mask //= 2
    return token_grad, final_plain(adasum_weights(gram)[:, order], lefts, rights, momentum)


def on_device(x_rows, row_cot, gate_vals, route_pos, weights, momentum):
    reps = lax.axis_size("rep")
    owners = lax.axis_size("exp")
    cap = x_rows.shape[1] // owners
    live = min(cap, route_pos.shape[1])
    width = x_rows.shape[2] // reps
    ff = weights.shape[3]
    sizes = (owners, cap, live, reps // 2, width, ff)
    body = with_kernels if kernels_fit(reps, owners, live, width, ff) else without_kernels
    return body(x_rows, row_cot, gate_vals, route_pos, weights, momentum, sizes)


def kernels_fit(reps, owners, live, width, ff):
    return width % 128 == 0 and ff % 128 == 0 and owners * live % 16 == 0 and reps == 8


def solution(mesh):
    placed = (
        P("rep", "exp", None),
        P("rep", "exp", None),
        P("rep", "exp"),
        P("rep", "exp", None),
        P("exp", None, None, None),
        P("exp", None, "rep", None),
    )
    return jax.shard_map(
        on_device,
        mesh=mesh,
        in_specs=placed,
        out_specs=(P("rep", "exp", None), P("exp", None, "rep", None)),
        check_vma=False,
    )
```

profile of v0, /device:TPU:0, one launch (start us, length us, event | category | flops | bytes accessed | tf_op | source)
XLA Modules:
  0.0 43.0 jit_solution(13275393459474455312)
XLA Ops:
  0.6 0.0 copy-start
  0.6 2.1 %pack.1 = (bf16[2,80,512]{2,1,0:T(8,128)(2,1)S(1)}, bf16[2,80,512]{2,1,0:T(8,128)(2,1)S(1)}, bf16[2,80,512]{2,1,0:T(8,128)(2,1)S(1)}, bf16[2,80,512]{2,1,0:T(8,128)(2,1)S(1)}) custom-call(bf16[1,128,2048]{2,1,0:T(8,128)(2,1)} %x_hbm.1, bf16[1,128,2048]{2,1,0:T(8,128)(2,1)} %cot_hbm.1, f32[1,128]{1,0:T(1,128)} %gate_hbm.1), custom_call_target="tpu_custom_call" | custom-call | flops 99999997952 | bytes 2097152 | tf_op jit(solution)/shard_map/pack/pallas_call | solution.py:94
  2.8 3.0 %collective-permute-start.11 = (bf16[2,80,512]{2,1,0:T(8,128)(2,1)S(1)}, bf16[2,80,512]{2,1,0:T(8,128)(2,1)S(1)}, u32[]{:S(2)}, u32[]{:S(2)}) collective-permute-start(bf16[2,80,512]{2,1,0:T(8,128)(2,1)S(1)} %get-tuple-element.13.refs_1_), channel_id=1, source_target_pairs={{0,8},{4,12},{8,0},{12,4},{16,24},{20,28},{24,16},{28,20},{1,9},{5... | collective-permute-start | bytes 491528 | tf_op jit(solution)/shard_map/ppermute | solution.py:21
  5.8 1.5 %collective-permute-start.13 = (bf16[2,80,512]{2,1,0:T(8,128)(2,1)S(1)}, bf16[2,80,512]{2,1,0:T(8,128)(2,1)S(1)}, u32[]{:S(2)}, u32[]{:S(2)}) collective-permute-start(bf16[2,80,512]{2,1,0:T(8,128)(2,1)S(1)} %get-tuple-element.14.refs_2_), channel_id=1, source_target_pairs={{0,16},{4,20},{8,24},{12,28},{16,0},{20,4},{24,8},{28,12},{1,17},{... | collective-permute-start | bytes 491528 | tf_op jit(solution)/shard_map/ppermute | solution.py:21
  7.3 0.0 collective-permute-start.15
  7.3 0.0 collective-permute-start.10
  7.4 0.9 %forward.1.small_ref.refs_0_ = bf16[80,1152]{1,0:T(8,128)(2,1)S(1)} custom-call(bf16[2,80,512]{2,1,0:T(8,128)(2,1)S(1)} %get-tuple-element.12.refs_0_, bf16[2,80,512]{2,1,0:T(8,128)(2,1)S(1)} %get-tuple-element.13.refs_1_, bf16[2,80,512]{2,1,0:T(8,128)(2,1)S(1)} %get-tuple-element.14.refs_2_, bf16[2,80,512]{2,1,0:T(8,128)(2,1)S(1)} %get-tuple-element.15.refs_3_, ...), custom_call_target="tpu_custom_call" | custom-call | flops 377487360 | bytes 4718592 | tf_op jit(solution)/shard_map/forward/pallas_call | solution.py:133
  8.3 2.0 %collective-permute-start.4 = (bf16[80,1152]{1,0:T(8,128)(2,1)S(1)}, bf16[80,1152]{1,0:T(8,128)(2,1)S(1)}, u32[]{:S(2)}, u32[]{:S(2)}) collective-permute-start(bf16[80,1152]{1,0:T(8,128)(2,1)S(1)} %forward.1.small_ref.refs_0_), channel_id=1, source_target_pairs={{0,8},{4,12},{8,0},{12,4},{16,24},{20,28},{24,16},{28,20},{1,9},{5... | collective-permute-start | bytes 552968 | tf_op jit(solution)/shard_map/ppermute | solution.py:21
  10.3 0.6 %collective-permute-done.11.refs_2_ = bf16[2,80,512]{2,1,0:T(8,128)(2,1)S(1)} collective-permute-done((bf16[2,80,512]{2,1,0:T(8,128)(2,1)S(1)}, bf16[2,80,512]{2,1,0:T(8,128)(2,1)S(1)}, u32[]{:S(2)}, u32[]{:S(2)}) %collective-permute-start.11) | collective-permute-done | bytes 163872 | tf_op jit(solution)/shard_map/ppermute | solution.py:21
  10.9 2.0 %collective-permute-start.6 = (bf16[80,1152]{1,0:T(8,128)(2,1)S(1)}, bf16[80,1152]{1,0:T(8,128)(2,1)S(1)}, u32[]{:S(2)}, u32[]{:S(2)}) collective-permute-start(bf16[80,1152]{1,0:T(8,128)(2,1)S(1)} %forward.1.small_ref.refs_0_), channel_id=1, source_target_pairs={{0,16},{4,20},{8,24},{12,28},{16,0},{20,4},{24,8},{28,12},{1,17},{... | collective-permute-start | bytes 552968 | tf_op jit(solution)/shard_map/ppermute | solution.py:21
  12.9 2.4 %collective-permute-done.13.refs_4_ = bf16[2,80,512]{2,1,0:T(8,128)(2,1)S(1)} collective-permute-done((bf16[2,80,512]{2,1,0:T(8,128)(2,1)S(1)}, bf16[2,80,512]{2,1,0:T(8,128)(2,1)S(1)}, u32[]{:S(2)}, u32[]{:S(2)}) %collective-permute-start.13) | collective-permute-done | bytes 163872 | tf_op jit(solution)/shard_map/ppermute | solution.py:21
  15.3 0.8 %collective-permute-start.8 = (bf16[80,1152]{1,0:T(8,128)(2,1)S(1)}, bf16[80,1152]{1,0:T(8,128)(2,1)S(1)}, u32[]{:S(2)}, u32[]{:S(2)}) collective-permute-start(bf16[80,1152]{1,0:T(8,128)(2,1)S(1)} %forward.1.small_ref.refs_0_), channel_id=1, source_target_pairs={{0,24},{4,28},{8,16},{12,20},{16,8},{20,12},{24,0},{28,4},{1,25},{... | collective-permute-start | bytes 552968 | tf_op jit(solution)/shard_map/ppermute | solution.py:21
  16.0 0.0 collective-permute-done.15.refs_6_
  16.0 0.0 collective-permute-start.12
  16.0 0.0 collective-permute-done.10.refs_1_
  16.0 0.5 %collective-permute-start.14 = (bf16[2,80,512]{2,1,0:T(8,128)(2,1)S(1)}, bf16[2,80,512]{2,1,0:T(8,128)(2,1)S(1)}, u32[]{:S(2)}, u32[]{:S(2)}) collective-permute-start(bf16[2,80,512]{2,1,0:T(8,128)(2,1)S(1)} %collective-permute-done.13.refs_4_), channel_id=1, source_target_pairs={{0,4},{4,0},{8,12},{12,8},{16,20},{20,16},{24,28},{28,24},{1,5},{5... | collective-permute-start | bytes 491528 | tf_op jit(solution)/shard_map/ppermute | solution.py:21
  16.5 1.8 %collective-permute-done.4.refs_2_ = bf16[80,1152]{1,0:T(8,128)(2,1)S(1)} collective-permute-done((bf16[80,1152]{1,0:T(8,128)(2,1)S(1)}, bf16[80,1152]{1,0:T(8,128)(2,1)S(1)}, u32[]{:S(2)}, u32[]{:S(2)}) %collective-permute-start.4) | collective-permute-done | bytes 184352 | tf_op jit(solution)/shard_map/ppermute | solution.py:21
  18.3 0.0 collective-permute-start.16
  18.3 4.5 %collective-permute-done.6.refs_4_ = bf16[80,1152]{1,0:T(8,128)(2,1)S(1)} collective-permute-done((bf16[80,1152]{1,0:T(8,128)(2,1)S(1)}, bf16[80,1152]{1,0:T(8,128)(2,1)S(1)}, u32[]{:S(2)}, u32[]{:S(2)}) %collective-permute-start.6) | collective-permute-done | bytes 184352 | tf_op jit(solution)/shard_map/ppermute | solution.py:21
  22.9 0.0 collective-permute-start.3
  22.9 0.0 collective-permute-done.8.refs_6_
  22.9 0.5 %collective-permute-start.5 = (bf16[80,1152]{1,0:T(8,128)(2,1)S(1)}, bf16[80,1152]{1,0:T(8,128)(2,1)S(1)}, u32[]{:S(2)}, u32[]{:S(2)}) collective-permute-start(bf16[80,1152]{1,0:T(8,128)(2,1)S(1)} %collective-permute-done.4.refs_2_), channel_id=1, source_target_pairs={{0,4},{4,0},{8,12},{12,8},{16,20},{20,16},{24,28},{28,24},{1,5},{5... | collective-permute-start | bytes 552968 | tf_op jit(solution)/shard_map/ppermute | solution.py:21
  23.4 0.0 collective-permute-done.12.refs_3_
  23.4 0.1 collective-permute-start.7
  23.5 0.0 collective-permute-done.14.refs_5_
  23.5 0.4 %collective-permute-start.9 = (bf16[80,1152]{1,0:T(8,128)(2,1)S(1)}, bf16[80,1152]{1,0:T(8,128)(2,1)S(1)}, u32[]{:S(2)}, u32[]{:S(2)}) collective-permute-start(bf16[80,1152]{1,0:T(8,128)(2,1)S(1)} %collective-permute-done.8.refs_6_), channel_id=1, source_target_pairs={{0,4},{4,0},{8,12},{12,8},{16,20},{20,16},{24,28},{28,24},{1,5},{5... | collective-permute-start | bytes 552968 | tf_op jit(solution)/shard_map/ppermute | solution.py:21
  23.9 1.2 %back.1 = (bf16[20,2048]{1,0:T(8,128)(2,1)S(1)}, bf16[20,2048]{1,0:T(8,128)(2,1)S(1)}, bf16[20,2048]{1,0:T(8,128)(2,1)S(1)}, bf16[20,2048]{1,0:T(8,128)(2,1)S(1)}) custom-call(bf16[80,1152]{1,0:T(8,128)(2,1)S(1)} %forward.1.small_ref.refs_0_, bf16[1,3,2048,384]{3,2,1,0:T(8,128)(2,1)S(1)} %copy-done), custom_call_target="tpu_custom_call" | custom-call | flops 251658240 | bytes 3145728 | tf_op jit(solution)/shard_map/back/pallas_call | solution.py:176
  25.1 0.0 collective-permute-done.16.refs_7_
  25.1 0.0 copy-start.2
  25.1 1.6 %collective-permute-start = (bf16[20,2048]{1,0:T(8,128)(2,1)S(1)}, bf16[20,2048]{1,0:T(8,128)(2,1)S(1)}, u32[]{:S(2)}, u32[]{:S(2)}) collective-permute-start(bf16[20,2048]{1,0:T(8,128)(2,1)S(1)} %get-tuple-element.17), channel_id=1, source_target_pairs={{0,1},{1,0},{2,3},{3,2},{4,5},{5,4},{6,7},{7,6},{8,9},{9,8},{10,11... | collective-permute-start | bytes 245768 | tf_op jit(solution)/shard_map/ppermute | solution.py:21
  26.8 1.2 %tall.1 = (f32[2,640,640]{2,1,0:T(8,128)S(1)}, bf16[2,256,640]{2,1,0:T(8,128)(2,1)S(1)}) custom-call(bf16[2,80,512]{2,1,0:T(8,128)(2,1)S(1)} %get-tuple-element.12.refs_0_, bf16[2,80,512]{2,1,0:T(8,128)(2,1)S(1)} %collective-permute-done.10.refs_1_, bf16[2,80,512]{2,1,0:T(8,128)(2,1)S(1)} %collective-permute-done.11.refs_2_, ...), custom_call_target="tpu_custom_call" | custom-call | flops 838860800 | bytes 5242880 | tf_op jit(solution)/shard_map/tall/pallas_call | solution.py:249
  28.0 0.0 copy-start.1
  28.0 0.0 collective-permute-done.3.refs_1_
  28.0 2.7 %collective-permute-start.1 = (bf16[20,2048]{1,0:T(8,128)(2,1)S(1)}, bf16[20,2048]{1,0:T(8,128)(2,1)S(1)}, u32[]{:S(2)}, u32[]{:S(2)}) collective-permute-start(bf16[20,2048]{1,0:T(8,128)(2,1)S(1)} %get-tuple-element.18), channel_id=1, source_target_pairs={{0,2},{1,3},{2,0},{3,1},{4,6},{5,7},{6,4},{7,5},{8,10},{9,11},{10,... | collective-permute-start | bytes 245768 | tf_op jit(solution)/shard_map/ppermute | solution.py:21
  30.7 0.0 collective-permute-done.5.refs_3_
  30.7 0.2 collective-permute-start.2
  30.9 0.0 collective-permute-done.7.refs_5_
  30.9 0.0 collective-permute-done.9.refs_7_
  30.9 2.4 %gram.1 = f32[24,128]{1,0:T(8,128)S(1)} custom-call(bf16[80,1152]{1,0:T(8,128)(2,1)S(1)} %forward.1.small_ref.refs_0_, bf16[80,1152]{1,0:T(8,128)(2,1)S(1)} %collective-permute-done.3.refs_1_, bf16[80,1152]{1,0:T(8,128)(2,1)S(1)} %collective-permute-done.4.refs_2_, bf16[80,1152]{1,0:T(8,128)(2,1)S(1)} %collective-permute-done.5.refs_3_, ...), custom_call_target="tpu_custom_call" | custom-call | flops 943718400 | bytes 4751360 | tf_op jit(solution)/shard_map/gram/pallas_call | solution.py:296
  33.3 1.6 %collective-permute-start.17 = (f32[24,128]{1,0:T(8,128)S(1)}, f32[24,128]{1,0:T(8,128)S(1)}, u32[]{:S(2)}, u32[]{:S(2)}) collective-permute-start(f32[24,128]{1,0:T(8,128)S(1)} %gram.1), channel_id=1, source_target_pairs={{0,16},{4,20},{8,24},{12,28},{16,0},{20,4},{24,8},{28,12},{1,17},{... | collective-permute-start | bytes 36872 | tf_op jit(solution)/shard_map/ppermute | solution.py:21
  34.9 2.2 %collective-permute-done.17 = f32[24,128]{1,0:T(8,128)S(1)} collective-permute-done((f32[24,128]{1,0:T(8,128)S(1)}, f32[24,128]{1,0:T(8,128)S(1)}, u32[]{:S(2)}, u32[]{:S(2)}) %collective-permute-start.17) | collective-permute-done | bytes 12320 | tf_op jit(solution)/shard_map/ppermute | solution.py:21
  37.1 0.8 %collective-permute-start.18 = (f32[24,128]{1,0:T(8,128)S(1)}, f32[24,128]{1,0:T(8,128)S(1)}, u32[]{:S(2)}, u32[]{:S(2)}) collective-permute-start(f32[24,128]{1,0:T(8,128)S(1)} %add.3.gram_ref), channel_id=1, source_target_pairs={{0,8},{4,12},{8,0},{12,4},{16,24},{20,28},{24,16},{28,20},{1,9},{5... | collective-permute-start | bytes 36872 | tf_op jit(solution)/shard_map/ppermute | solution.py:21
  37.9 0.0 collective-permute-done.refs_1_
  37.9 0.3 collective-permute-done.1.refs_2_
  38.2 0.0 collective-permute-done.2.refs_3_
  38.2 0.9 %token_.1 = bf16[1,20,2048]{2,1,0:T(8,128)(2,1)} custom-call(s32[1,4,20]{2,1,0:T(4,128)S(1)} %bitcast.1, bf16[20,2048]{1,0:T(8,128)(2,1)S(1)} %get-tuple-element.16.refs_0_, bf16[20,2048]{1,0:T(8,128)(2,1)S(1)} %collective-permute-done.refs_1_, bf16[20,2048]{1,0:T(8,128)(2,1)S(1)} %collective-permute-done.1.refs_2_, ...), custom_call_target="tpu_custom_call" | custom-call | flops 10485760 | bytes 655360 | tf_op jit(solution)/shard_map/token/pallas_call | solution.py:215
  39.1 1.6 %collective-permute-done.18.other_ref = f32[24,128]{1,0:T(8,128)S(1)} collective-permute-done((f32[24,128]{1,0:T(8,128)S(1)}, f32[24,128]{1,0:T(8,128)S(1)}, u32[]{:S(2)}, u32[]{:S(2)}) %collective-permute-start.18) | collective-permute-done | bytes 12320 | tf_op jit(solution)/shard_map/ppermute | solution.py:21
  40.8 2.2 %final.1 = f32[1,3,256,384]{3,2,1,0:T(8,128)} custom-call(f32[24,128]{1,0:T(8,128)S(1)} %add.3.gram_ref, f32[24,128]{1,0:T(8,128)S(1)} %collective-permute-done.18.other_ref, bf16[2,256,640]{2,1,0:T(8,128)(2,1)S(1)} %get-tuple-element.21.flip_ref, bf16[80,1152]{1,0:T(8,128)(2,1)S(1)} %forward.1.small_ref.refs_0_, ...), custom_call_target="tpu_custom_call" | custom-call | flops 377487360 | bytes 3833856 | tf_op jit(solution)/shard_map/final/pallas_call | solution.py:354
  (4 shorter events, 0.0 us)
Async XLA Ops:
  0.6 6.7 %copy-start = (bf16[1,3,2048,384]{3,2,1,0:T(8,128)(2,1)S(1)}, bf16[1,3,2048,384]{3,2,1,0:T(8,128)(2,1)}, u32[]{:S(2)}) copy-start(bf16[1,3,2048,384]{3,2,1,0:T(8,128)(2,1)} %w_ref.1) | copy-start | bytes 14155780
  2.8 8.1 %collective-permute-start.11 = (bf16[2,80,512]{2,1,0:T(8,128)(2,1)S(1)}, bf16[2,80,512]{2,1,0:T(8,128)(2,1)S(1)}, u32[]{:S(2)}, u32[]{:S(2)}) collective-permute-start(bf16[2,80,512]{2,1,0:T(8,128)(2,1)S(1)} %get-tuple-element.13.refs_1_), channel_id=1, source_target_pairs={{0,8},{4,12},{8,0},{12,4},{16,24},{20,28},{24,16},{28,20},{1,9},{5... | collective-permute-start | bytes 491528 | tf_op jit(solution)/shard_map/ppermute | solution.py:21
  5.8 9.4 %collective-permute-start.13 = (bf16[2,80,512]{2,1,0:T(8,128)(2,1)S(1)}, bf16[2,80,512]{2,1,0:T(8,128)(2,1)S(1)}, u32[]{:S(2)}, u32[]{:S(2)}) collective-permute-start(bf16[2,80,512]{2,1,0:T(8,128)(2,1)S(1)} %get-tuple-element.14.refs_2_), channel_id=1, source_target_pairs={{0,16},{4,20},{8,24},{12,28},{16,0},{20,4},{24,8},{28,12},{1,17},{... | collective-permute-start | bytes 491528 | tf_op jit(solution)/shard_map/ppermute | solution.py:21
  7.3 8.7 %collective-permute-start.15 = (bf16[2,80,512]{2,1,0:T(8,128)(2,1)S(1)}, bf16[2,80,512]{2,1,0:T(8,128)(2,1)S(1)}, u32[]{:S(2)}, u32[]{:S(2)}) collective-permute-start(bf16[2,80,512]{2,1,0:T(8,128)(2,1)S(1)} %get-tuple-element.15.refs_3_), channel_id=1, source_target_pairs={{0,24},{4,28},{8,16},{12,20},{16,8},{20,12},{24,0},{28,4},{1,25},{... | collective-permute-start | bytes 491528 | tf_op jit(solution)/shard_map/ppermute | solution.py:21
  7.3 8.7 %collective-permute-start.10 = (bf16[2,80,512]{2,1,0:T(8,128)(2,1)S(1)}, bf16[2,80,512]{2,1,0:T(8,128)(2,1)S(1)}, u32[]{:S(2)}, u32[]{:S(2)}) collective-permute-start(bf16[2,80,512]{2,1,0:T(8,128)(2,1)S(1)} %get-tuple-element.12.refs_0_), channel_id=1, source_target_pairs={{0,4},{4,0},{8,12},{12,8},{16,20},{20,16},{24,28},{28,24},{1,5},{5... | collective-permute-start | bytes 491528 | tf_op jit(solution)/shard_map/ppermute | solution.py:21
  8.3 10.1 %collective-permute-start.4 = (bf16[80,1152]{1,0:T(8,128)(2,1)S(1)}, bf16[80,1152]{1,0:T(8,128)(2,1)S(1)}, u32[]{:S(2)}, u32[]{:S(2)}) collective-permute-start(bf16[80,1152]{1,0:T(8,128)(2,1)S(1)} %forward.1.small_ref.refs_0_), channel_id=1, source_target_pairs={{0,8},{4,12},{8,0},{12,4},{16,24},{20,28},{24,16},{28,20},{1,9},{5... | collective-permute-start | bytes 552968 | tf_op jit(solution)/shard_map/ppermute | solution.py:21
  10.9 12.0 %collective-permute-start.6 = (bf16[80,1152]{1,0:T(8,128)(2,1)S(1)}, bf16[80,1152]{1,0:T(8,128)(2,1)S(1)}, u32[]{:S(2)}, u32[]{:S(2)}) collective-permute-start(bf16[80,1152]{1,0:T(8,128)(2,1)S(1)} %forward.1.small_ref.refs_0_), channel_id=1, source_target_pairs={{0,16},{4,20},{8,24},{12,28},{16,0},{20,4},{24,8},{28,12},{1,17},{... | collective-permute-start | bytes 552968 | tf_op jit(solution)/shard_map/ppermute | solution.py:21
  15.3 7.6 %collective-permute-start.8 = (bf16[80,1152]{1,0:T(8,128)(2,1)S(1)}, bf16[80,1152]{1,0:T(8,128)(2,1)S(1)}, u32[]{:S(2)}, u32[]{:S(2)}) collective-permute-start(bf16[80,1152]{1,0:T(8,128)(2,1)S(1)} %forward.1.small_ref.refs_0_), channel_id=1, source_target_pairs={{0,24},{4,28},{8,16},{12,20},{16,8},{20,12},{24,0},{28,4},{1,25},{... | collective-permute-start | bytes 552968 | tf_op jit(solution)/shard_map/ppermute | solution.py:21
  16.0 7.4 %collective-permute-start.12 = (bf16[2,80,512]{2,1,0:T(8,128)(2,1)S(1)}, bf16[2,80,512]{2,1,0:T(8,128)(2,1)S(1)}, u32[]{:S(2)}, u32[]{:S(2)}) collective-permute-start(bf16[2,80,512]{2,1,0:T(8,128)(2,1)S(1)} %collective-permute-done.11.refs_2_), channel_id=1, source_target_pairs={{0,4},{4,0},{8,12},{12,8},{16,20},{20,16},{24,28},{28,24},{1,5},{5... | collective-permute-start | bytes 491528 | tf_op jit(solution)/shard_map/ppermute | solution.py:21
  16.0 7.4 %collective-permute-start.14 = (bf16[2,80,512]{2,1,0:T(8,128)(2,1)S(1)}, bf16[2,80,512]{2,1,0:T(8,128)(2,1)S(1)}, u32[]{:S(2)}, u32[]{:S(2)}) collective-permute-start(bf16[2,80,512]{2,1,0:T(8,128)(2,1)S(1)} %collective-permute-done.13.refs_4_), channel_id=1, source_target_pairs={{0,4},{4,0},{8,12},{12,8},{16,20},{20,16},{24,28},{28,24},{1,5},{5... | collective-permute-start | bytes 491528 | tf_op jit(solution)/shard_map/ppermute | solution.py:21
  18.3 6.8 %collective-permute-start.16 = (bf16[2,80,512]{2,1,0:T(8,128)(2,1)S(1)}, bf16[2,80,512]{2,1,0:T(8,128)(2,1)S(1)}, u32[]{:S(2)}, u32[]{:S(2)}) collective-permute-start(bf16[2,80,512]{2,1,0:T(8,128)(2,1)S(1)} %collective-permute-done.15.refs_6_), channel_id=1, source_target_pairs={{0,4},{4,0},{8,12},{12,8},{16,20},{20,16},{24,28},{28,24},{1,5},{5... | collective-permute-start | bytes 491528 | tf_op jit(solution)/shard_map/ppermute | solution.py:21
  22.9 5.1 %collective-permute-start.3 = (bf16[80,1152]{1,0:T(8,128)(2,1)S(1)}, bf16[80,1152]{1,0:T(8,128)(2,1)S(1)}, u32[]{:S(2)}, u32[]{:S(2)}) collective-permute-start(bf16[80,1152]{1,0:T(8,128)(2,1)S(1)} %forward.1.small_ref.refs_0_), channel_id=1, source_target_pairs={{0,4},{4,0},{8,12},{12,8},{16,20},{20,16},{24,28},{28,24},{1,5},{5... | collective-permute-start | bytes 552968 | tf_op jit(solution)/shard_map/ppermute | solution.py:21
  22.9 7.8 %collective-permute-start.5 = (bf16[80,1152]{1,0:T(8,128)(2,1)S(1)}, bf16[80,1152]{1,0:T(8,128)(2,1)S(1)}, u32[]{:S(2)}, u32[]{:S(2)}) collective-permute-start(bf16[80,1152]{1,0:T(8,128)(2,1)S(1)} %collective-permute-done.4.refs_2_), channel_id=1, source_target_pairs={{0,4},{4,0},{8,12},{12,8},{16,20},{20,16},{24,28},{28,24},{1,5},{5... | collective-permute-start | bytes 552968 | tf_op jit(solution)/shard_map/ppermute | solution.py:21
  23.4 7.5 %collective-permute-start.7 = (bf16[80,1152]{1,0:T(8,128)(2,1)S(1)}, bf16[80,1152]{1,0:T(8,128)(2,1)S(1)}, u32[]{:S(2)}, u32[]{:S(2)}) collective-permute-start(bf16[80,1152]{1,0:T(8,128)(2,1)S(1)} %collective-permute-done.6.refs_4_), channel_id=1, source_target_pairs={{0,4},{4,0},{8,12},{12,8},{16,20},{20,16},{24,28},{28,24},{1,5},{5... | collective-permute-start | bytes 552968 | tf_op jit(solution)/shard_map/ppermute | solution.py:21
  23.5 7.4 %collective-permute-start.9 = (bf16[80,1152]{1,0:T(8,128)(2,1)S(1)}, bf16[80,1152]{1,0:T(8,128)(2,1)S(1)}, u32[]{:S(2)}, u32[]{:S(2)}) collective-permute-start(bf16[80,1152]{1,0:T(8,128)(2,1)S(1)} %collective-permute-done.8.refs_6_), channel_id=1, source_target_pairs={{0,4},{4,0},{8,12},{12,8},{16,20},{20,16},{24,28},{28,24},{1,5},{5... | collective-permute-start | bytes 552968 | tf_op jit(solution)/shard_map/ppermute | solution.py:21
  25.1 13.1 %copy-start.2 = (s32[1,20,4]{1,2,0:T(4,128)S(1)}, s32[1,20,4]{1,2,0:T(4,128)}, u32[]{:S(2)}) copy-start(s32[1,20,4]{1,2,0:T(4,128)} %param.9) | copy-start | bytes 964
  25.1 12.8 %collective-permute-start = (bf16[20,2048]{1,0:T(8,128)(2,1)S(1)}, bf16[20,2048]{1,0:T(8,128)(2,1)S(1)}, u32[]{:S(2)}, u32[]{:S(2)}) collective-permute-start(bf16[20,2048]{1,0:T(8,128)(2,1)S(1)} %get-tuple-element.17), channel_id=1, source_target_pairs={{0,1},{1,0},{2,3},{3,2},{4,5},{5,4},{6,7},{7,6},{8,9},{9,8},{10,11... | collective-permute-start | bytes 245768 | tf_op jit(solution)/shard_map/ppermute | solution.py:21
  28.0 12.8 %copy-start.1 = (f32[1,3,256,384]{3,2,1,0:T(8,128)S(1)}, f32[1,3,256,384]{3,2,1,0:T(8,128)}, u32[]{:S(2)}) copy-start(f32[1,3,256,384]{3,2,1,0:T(8,128)} %refs_8_.1) | copy-start | bytes 3538948
  28.0 10.2 %collective-permute-start.1 = (bf16[20,2048]{1,0:T(8,128)(2,1)S(1)}, bf16[20,2048]{1,0:T(8,128)(2,1)S(1)}, u32[]{:S(2)}, u32[]{:S(2)}) collective-permute-start(bf16[20,2048]{1,0:T(8,128)(2,1)S(1)} %get-tuple-element.18), channel_id=1, source_target_pairs={{0,2},{1,3},{2,0},{3,1},{4,6},{5,7},{6,4},{7,5},{8,10},{9,11},{10,... | collective-permute-start | bytes 245768 | tf_op jit(solution)/shard_map/ppermute | solution.py:21
  30.7 7.5 %collective-permute-start.2 = (bf16[20,2048]{1,0:T(8,128)(2,1)S(1)}, bf16[20,2048]{1,0:T(8,128)(2,1)S(1)}, u32[]{:S(2)}, u32[]{:S(2)}) collective-permute-start(bf16[20,2048]{1,0:T(8,128)(2,1)S(1)} %get-tuple-element.19), channel_id=1, source_target_pairs={{0,3},{1,2},{2,1},{3,0},{4,7},{5,6},{6,5},{7,4},{8,11},{9,10},{10,... | collective-permute-start | bytes 245768 | tf_op jit(solution)/shard_map/ppermute | solution.py:21
  33.3 3.8 %collective-permute-start.17 = (f32[24,128]{1,0:T(8,128)S(1)}, f32[24,128]{1,0:T(8,128)S(1)}, u32[]{:S(2)}, u32[]{:S(2)}) collective-permute-start(f32[24,128]{1,0:T(8,128)S(1)} %gram.1), channel_id=1, source_target_pairs={{0,16},{4,20},{8,24},{12,28},{16,0},{20,4},{24,8},{28,12},{1,17},{... | collective-permute-start | bytes 36872 | tf_op jit(solution)/shard_map/ppermute | solution.py:21
  37.1 3.7 %collective-permute-start.18 = (f32[24,128]{1,0:T(8,128)S(1)}, f32[24,128]{1,0:T(8,128)S(1)}, u32[]{:S(2)}, u32[]{:S(2)}) collective-permute-start(f32[24,128]{1,0:T(8,128)S(1)} %add.3.gram_ref), channel_id=1, source_target_pairs={{0,8},{4,12},{8,0},{12,4},{16,24},{20,28},{24,16},{28,20},{1,9},{5... | collective-permute-start | bytes 36872 | tf_op jit(solution)/shard_map/ppermute | solution.py:21
where the time goes:
time: 43.1 us; the launch traced here: 43 us
  starting transfers between devices  17.9 us (42%)
  waiting for transfers between devices  13.4 us (31%)
  Pallas kernels  11 us (26%)
  between operations  0.73 us (2%)
    ppermute x19, starting transfers between devices, swap(): return lax.ppermute(block, axis, [(i, i ^ mask) for i in range(count)])  17.9 us
    ppermute x19, waiting for transfers between devices, swap(): return lax.ppermute(block, axis, [(i, i ^ mask) for i in range(count)])  13.4 us
    pallas_call x1, Pallas kernels, gram_call(): pl.pallas_call(functools.partial(gram_kernel, reps, ff), out_shape=jax.Sh...  2.41 us
    pallas_call x1, Pallas kernels, final_call(): pl.pallas_call(functools.partial(final_kernel, reps, ff), out_shape=jax.S...  2.23 us
    pallas_call x1, Pallas kernels, pack_call(): pl.pallas_call(functools.partial(pack_kernel, sizes), out_shape=[jax.Shap...  2.13 us
    pallas_call x1, Pallas kernels, tall_call(): pl.pallas_call(functools.partial(tall_kernel, reps), out_shape=[jax.Shape...  1.22 us
    pallas_call x1, Pallas kernels, back_call(): pl.pallas_call(functools.partial(back_kernel, sizes), out_shape=[jax.Shap...  1.17 us
    pallas_call x1, Pallas kernels, forward_call(): pl.pallas_call(functools.partial(forward_kernel, sizes), out_shape=jax.Sh...  0.92 us
  transfers between devices with their start and end apart: 19, of which 7 were waited for; matrix products, arithmetic and copies ran while one was open for 0% of the time, Pallas kernels for 15%

commit v1 on v0

--- a/solution.py
+++ b/solution.py
@@ -19,6 +19,27 @@
 def swap(block, axis, mask):
     count = lax.axis_size(axis)
     return lax.ppermute(block, axis, [(i, i ^ mask) for i in range(count)])
+
+
+def turn_step(core, turn):
+    return turn if turn in (0, 3) else turn ^ 3 ^ (3 * core)
+
+
+def turn_swap(block, turn):
+    count = lax.axis_size("rep")
+    route = [(i, i ^ (2 * turn_step(i & 1, turn))) for i in range(count)]
+    return lax.ppermute(block, "rep", route)
+
+
+block_order = (0, 1, 2, 4, 6, 3, 5, 7)
+late_blocks = 3
+
+
+def replica_of(me, place):
+    core, block = me & 1, block_order[place]
+    if block & 1:
+        core, me = 1 - core, me ^ 1
+    return me ^ (2 * turn_step(core, block >> 1))
 
 
 def live_rows(block, owners, live):
@@ -60,12 +81,13 @@
     owners, cap, live, chips, width, _ = sizes
     out_refs, (x_ref, cot_ref, gate_ref, sems, gate_sem) = refs[:chips], refs[chips:]
     slots, rows = owners * cap, owners * live
-    chip = lax.axis_index("rep") >> 1
+    me = lax.axis_index("rep")
     gate_copy = pltpu.make_async_copy(gate_hbm, gate_ref, gate_sem)
     gate_copy.start()
     copies = []
     for k in range(chips):
-        at = pl.ds(pl.multiple_of((chip ^ k) * 2 * width, 2 * width), 2 * width)
+        chip = (me >> 1) ^ turn_step(me & 1, k)
+        at = pl.ds(pl.multiple_of(chip * 2 * width, 2 * width), 2 * width)
         for side, (source, target) in enumerate([(x_hbm, x_ref), (cot_hbm, cot_ref)]):
             copy = pltpu.make_async_copy(source.at[0, :, at], target.at[k], sems.at[k, side])
             copy.start()
@@ -114,11 +136,12 @@
 def forward_kernel(sizes, *refs):
     _, _, _, chips, width, ff = sizes
     pair_refs, w_ref, small_ref = refs[:chips], refs[chips], refs[chips + 1]
-    chip = lax.axis_index("rep") >> 1
+    me = lax.axis_index("rep")
     sums = [None] * 3
     for k in range(chips):
+        chip = (me >> 1) ^ turn_step(me & 1, k)
         for core in range(2):
-            at = pl.ds(pl.multiple_of(((chip ^ k) * 2 + core) * width, width), width)
+            at = pl.ds(pl.multiple_of((chip * 2 + core) * width, width), width)
             for t in range(3):
                 left = pair_refs[k][core, :, width:] if t == 2 else pair_refs[k][core, :, :width]
                 part = jnp.dot(left, w_ref[0, t, at, :], preferred_element_type=f32)
@@ -264,59 +287,105 @@
     )(*tall)
 
 
-def gram_kernel(reps, ff, *refs):
-    wide_refs, tall_ref, out_ref = refs[:reps], refs[reps], refs[reps + 1]
-    rows = wide_refs[0].shape[0]
+def pair_sums(wide_refs, tall_ref, ff, me, start):
+    reps, rows = len(wide_refs), wide_refs[0].shape[0]
     flat = reps * rows
-    me = lax.axis_index("rep")
     spot = lax.broadcasted_iota(jnp.int32, (flat, 128), 0)
     lane = lax.broadcasted_iota(jnp.int32, (flat, 128), 1)
-    group = jnp.zeros_like(spot)
+    group = jnp.full_like(spot, me)
     for k in range(1, reps):
-        group = group + jnp.where(spot >= k * rows, 1, 0)
-    gather = jnp.where((group ^ me) == (lane & (reps - 1)), 1.0, 0.0)
+        group = jnp.where(spot >= k * rows, replica_of(me, k), group)
+    gather = jnp.where(group == (lane & 7), 1.0, 0.0)
     sums = []
     for t in range(3):
         block = jnp.concatenate([ref[:, t * ff : (t + 1) * ff] for ref in wide_refs], axis=0)
-        both = lax.dot_general(block, block, contract_cols, preferred_element_type=f32)
-        both = both * tall_ref[t // 2]
-        sums.append(jnp.sum(both.reshape(reps, rows // 8, 8, flat), axis=1).reshape(reps * 8, flat))
+        both = lax.dot_general(
+            block[start * rows :], block, contract_cols, preferred_element_type=f32
+        )
+        both = both * tall_ref[t // 2, start * rows : flat, :flat]
+        both = both.reshape(reps - start, rows // 8, 8, flat)
+        sums.append(jnp.sum(both, axis=1).reshape((reps - start) * 8, flat))
     sums = jnp.dot(
         jnp.concatenate(sums, axis=0), gather, precision=HIGHEST, preferred_element_type=f32
     )
-    sums = jnp.sum(sums.reshape(3 * reps, 8, 128), axis=1)
+    return jnp.sum(sums.reshape(3 * (reps - start), 8, 128), axis=1)
+
+
+def first_kernel(reps, ff, *refs):
+    wide_refs, tall_ref, out_ref = refs[:-2], refs[-2], refs[-1]
+    me, count = lax.axis_index("rep"), len(wide_refs)
+    sums = pair_sums(wide_refs, tall_ref, ff, me, 0)
+    out_ref[...] = jnp.zeros_like(out_ref)
     for t in range(3):
-        for k in range(reps):
-            out_ref[pl.ds(t * reps + (me ^ k), 1), :] = sums[t * reps + k : t * reps + k + 1]
-
-
-def gram_call(wide, tall_gram, ff):
+        for k in range(count):
+            at = pl.ds(t * reps + replica_of(me, k), 1)
+            out_ref[at, :] = sums[t * count + k : t * count + k + 1]
+
+
+def last_kernel(reps, ff, *refs):
+    wide_refs, tall_ref, first_ref, out_ref = refs[:reps], refs[reps], refs[reps + 1], refs[reps + 2]
+    me = lax.axis_index("rep")
+    sums = pair_sums(wide_refs, tall_ref, ff, me, reps - late_blocks)
+    line = lax.broadcasted_iota(jnp.int32, (reps, 128), 0)
+    lane = lax.broadcasted_iota(jnp.int32, (reps, 128), 1)
+    near = lane & (reps - 1)
+    owns = [replica_of(me, k) for k in range(reps - late_blocks, reps)]
+    old = line >= 0
+    for own in owns:
+        old = old & (line != own)
+    for t in range(3):
+        gram = first_ref[t * reps : (t + 1) * reps, :]
+        for j, own in enumerate(owns):
+            row = jnp.broadcast_to(sums[late_blocks * t + j : late_blocks * t + j + 1], (reps, 128))
+            column = jnp.sum(jnp.where(line == lane, row, 0.0), axis=1, keepdims=True)
+            gram = gram + jnp.where(line == own, row, 0.0)
+            gram = gram + jnp.where(old & (near == own), column, 0.0)
+        out_ref[t * reps : (t + 1) * reps, :] = gram
+
+
+def gram_calls(wide, tall_gram, ff):
     reps, rows = len(wide), wide[0].shape[0]
     flat = reps * rows
-    return pl.pallas_call(
-        functools.partial(gram_kernel, reps, ff),
-        out_shape=jax.ShapeDtypeStruct((3 * reps, 128), f32),
-        in_specs=[VMEM] * (reps + 1),
+    shape = jax.ShapeDtypeStruct((3 * reps, 128), f32)
+    first = pl.pallas_call(
+        functools.partial(first_kernel, reps, ff),
+        out_shape=shape,
+        in_specs=[VMEM] * (reps - late_blocks + 1),
         out_specs=VMEM,
         compiler_params=kernel_params(6),
         cost_estimate=pl.CostEstimate(
-            flops=6 * flat * flat * ff,
-            bytes_accessed=8 * flat * flat + 6 * flat * ff,
+            flops=3 * flat * flat * ff,
+            bytes_accessed=4 * flat * flat + 4 * flat * ff,
             transcendentals=0,
         ),
-        name="gram",
-    )(*wide, tall_gram)
-
-
-def final_kernel(reps, ff, gram_ref, other_ref, flip_ref, *refs):
-    wide_refs, moment_ref, out_ref, coef_ref = refs[:reps], refs[reps], refs[reps + 1], refs[reps + 2]
+        name="first",
+    )(*wide[:-late_blocks], tall_gram)
+    return pl.pallas_call(
+        functools.partial(last_kernel, reps, ff),
+        out_shape=shape,
+        in_specs=[VMEM] * (reps + 2),
+        out_specs=VMEM,
+        compiler_params=kernel_params(6),
+        cost_estimate=pl.CostEstimate(
+            flops=3 * flat * flat * ff // 2,
+            bytes_accessed=2 * flat * flat + 6 * flat * ff,
+            transcendentals=0,
+        ),
+        name="last",
+    )(*wide, tall_gram, first)
+
+
+def final_kernel(reps, ff, *refs):
+    gram_refs, flip_ref, refs = refs[:2], refs[2], refs[3:]
+    wide_refs, (moment_ref, out_hbm, coef_ref, out_ref, sems) = refs[:reps], refs[reps:]
+    copies = []
     me = lax.axis_index("rep")
     line = lax.broadcasted_iota(jnp.int32, (reps, 128), 0)
     lane = lax.broadcasted_iota(jnp.int32, (reps, 128), 1)
     near = lane & (reps - 1)
     for t in range(3):
         part = slice(t * reps, (t + 1) * reps)
-        gram = gram_ref[part, :] + other_ref[part, :]
+        gram = gram_refs[0][part, :] + gram_refs[1][part, :]
         coefs = jnp.ones((reps, 128), f32)
         half = reps // 2
         while half >= 1:
@@ -341,22 +410,30 @@
     for t in range(3):
         scaled = []
         for k in range(reps):
-            coef = coef_ref[pl.ds(t * reps + (me ^ k), 1), :]
+            coef = coef_ref[pl.ds(t * reps + replica_of(me, k), 1), :]
             scaled.append((coef * wide_refs[k][:, t * ff : (t + 1) * ff].astype(f32)).astype(bf16))
         combined = jnp.dot(
             flip_ref[t // 2], jnp.concatenate(scaled, axis=0), preferred_element_type=f32
         )
         out_ref[0, t] = moment_decay * moment_ref[0, t] + (1.0 - moment_decay) * combined
-
-
-def final_call(gram, other, flip, wide, momentum, ff):
+        copies.append(pltpu.make_async_copy(out_ref.at[0, t], out_hbm.at[0, t], sems.at[t]))
+        copies[t].start()
+    for copy in copies:
+        copy.wait()
+
+
+def final_call(grams, flip, wide, momentum, ff):
     reps, rows = len(wide), wide[0].shape[0]
     return pl.pallas_call(
         functools.partial(final_kernel, reps, ff),
         out_shape=jax.ShapeDtypeStruct(momentum.shape, f32),
-        in_specs=[VMEM] * (reps + 4),
-        out_specs=VMEM,
-        scratch_shapes=[pltpu.VMEM((3 * reps, ff), f32)],
+        in_specs=[VMEM] * (len(grams) + reps + 2),
+        out_specs=HBM,
+        scratch_shapes=[
+            pltpu.VMEM((3 * reps, ff), f32),
+            pltpu.VMEM(momentum.shape, f32),
+            pltpu.SemaphoreType.DMA((3,)),
+        ],
         compiler_params=kernel_params(6),
         cost_estimate=pl.CostEstimate(
             flops=2 * reps * rows * momentum.size,
@@ -364,7 +441,7 @@
             transcendentals=0,
         ),
         name="final",
-    )(gram, other, flip, *wide, momentum)
+    )(*grams, flip, *wide, momentum)
 
 
 def adasum_weights(gram):
@@ -441,10 +518,10 @@
     return jnp.dot(picks.astype(bf16), returned, preferred_element_type=f32).astype(bf16)[None]
 
 
-def all_swaps(blocks, axis, scale):
-    got = []
-    for k, block in enumerate(blocks):
-        got.append(swap(block, axis, k * scale) if k else block)
+def turns(blocks):
+    got = [blocks[0]]
+    for k in range(1, len(blocks)):
+        got.append(turn_swap(blocks[k], k))
     return got
 
 
@@ -452,26 +529,25 @@
     got = []
     for mine in blocks:
         got += [mine, swap(mine, "rep", 1)]
-    return got
+    return [got[block] for block in block_order]
 
 
 def with_kernels(x_rows, row_cot, gate_vals, route_pos, weights, momentum, sizes):
-    _, cap, _, chips, _, ff = sizes
+    owners, cap, _, chips, _, ff = sizes
     pairs = pack_call(x_rows, row_cot, gate_vals, sizes)
-    tall = all_swaps(pairs, "rep", 2)
+    tall = turns(pairs)
     small = forward_call(pairs, weights, sizes)
-    wide = all_swaps([small] * chips, "rep", 2)
-    returned = all_swaps(back_call(small, weights, sizes), "exp", 1)
+    wide = turns([small] * chips)
+    returned = list(back_call(small, weights, sizes))
+    for k in range(1, owners):
+        returned[k] = swap(returned[k], "exp", k)
     token_grad = token_call(route_pos, returned, cap)
     tall, wide = core_swaps(tall), core_swaps(wide)
     tall_gram, flip = tall_call(tall)
-    gram = gram_call(wide, tall_gram, ff)
-    mask = chips
-    while mask > 2:
-        gram = gram + swap(gram, "rep", mask)
-        mask //= 2
-    other = swap(gram, "rep", 2)
-    return token_grad, final_call(gram, other, flip, wide, momentum, ff)
+    gram = gram_calls(wide, tall_gram, ff)
+    gram = gram + swap(gram, "rep", 4)
+    grams = [gram, swap(gram, "rep", 2)]
+    return token_grad, final_call(grams, flip, wide, momentum, ff)
 
 
 def without_kernels(x_rows, row_cot, gate_vals, route_pos, weights, momentum, sizes):
@@ -479,7 +555,8 @@
     reps = 2 * chips
     slices, small = forward_plain(x_rows, row_cot, gate_vals, weights, sizes)
     tall = lax.all_to_all(slices, "rep", split_axis=0, concat_axis=0, tiled=True)
-    wide = jnp.stack(core_swaps(all_swaps([small] * chips, "rep", 2)))
+    wide = [swap(small, "rep", k) if k else small for k in range(reps)]
+    wide = jnp.stack(wide)
     returned = back_plain(small, weights, sizes)
     returned = lax.all_to_all(returned, "exp", split_axis=0, concat_axis=0, tiled=True)
     token_grad = token_plain(route_pos, returned, cap)

time: 43.1 us -> 43 us (level)
  starting transfers between devices: 17.9 us -> 19.8 us
  waiting for transfers between devices: 13.4 us -> 11.5 us
    ppermute x0 -> x6, starting transfers between devices: none -> 10.9 us  [turn_swap(): return lax.ppermute(block, 'rep', route)]
    ppermute x19 -> x13, waiting for transfers between devices: 13.4 us -> 4.39 us  [swap(): return lax.ppermute(block, axis, [(i, i ^ mask) for i in range(count)])]
    ppermute x19 -> x13, starting transfers between devices: 17.9 us -> 8.95 us  [swap(): return lax.ppermute(block, axis, [(i, i ^ mask) for i in range(count)])]
    ppermute x0 -> x6, waiting for transfers between devices: none -> 7.11 us  [turn_swap(): return lax.ppermute(block, 'rep', route)]
    pallas_call x1 -> x2, Pallas kernels: 2.41 us -> 2.42 us  [the longest x1 1.21 us: gram_calls(): pl.pallas_call(functools.partial(first_kernel, reps, ff), out_shape=shape...]
  transfers between devices with their start and end apart: 19 -> 19, of which waited for: 7 -> 6; matrix products, arithmetic and copies ran while one was open for 0% -> 0% of each run, Pallas kernels for 15% -> 16%
where the time goes in v1:
time: 43 us; the launch traced here: 42.8 us
  starting transfers between devices  19.8 us (46%)
  waiting for transfers between devices  11.5 us (27%)
  Pallas kernels  10.8 us (25%)
  between operations  0.74 us (2%)
    ppermute x6, starting transfers between devices, turn_swap(): return lax.ppermute(block, 'rep', route)  10.9 us
    ppermute x13, starting transfers between devices, swap(): return lax.ppermute(block, axis, [(i, i ^ mask) for i in range(count)])  8.95 us
    ppermute x6, waiting for transfers between devices, turn_swap(): return lax.ppermute(block, 'rep', route)  7.11 us
    ppermute x13, waiting for transfers between devices, swap(): return lax.ppermute(block, axis, [(i, i ^ mask) for i in range(count)])  4.39 us
    pallas_call x1, Pallas kernels, pack_call(): pl.pallas_call(functools.partial(pack_kernel, sizes), out_shape=[jax.Shap...  2.13 us
    pallas_call x1, Pallas kernels, final_call(): pl.pallas_call(functools.partial(final_kernel, reps, ff), out_shape=jax.S...  1.99 us
    pallas_call x1, Pallas kernels, tall_call(): pl.pallas_call(functools.partial(tall_kernel, reps), out_shape=[jax.Shape...  1.22 us
    pallas_call x1, Pallas kernels, gram_calls(): pl.pallas_call(functools.partial(first_kernel, reps, ff), out_shape=shape...  1.21 us
  transfers between devices with their start and end apart: 19, of which 6 were waited for; matrix products, arithmetic and copies ran while one was open for 0% of the time, Pallas kernels for 16%

profile of v1, /device:TPU:0, one launch (start us, length us, event | category | flops | bytes accessed | tf_op | source)
XLA Modules:
  0.0 42.8 jit_solution(5239216472613244338)
XLA Ops:
  0.6 2.1 %pack.1 = (bf16[2,80,512]{2,1,0:T(8,128)(2,1)S(1)}, bf16[2,80,512]{2,1,0:T(8,128)(2,1)S(1)}, bf16[2,80,512]{2,1,0:T(8,128)(2,1)S(1)}, bf16[2,80,512]{2,1,0:T(8,128)(2,1)S(1)}) custom-call(bf16[1,128,2048]{2,1,0:T(8,128)(2,1)} %x_hbm.1, bf16[1,128,2048]{2,1,0:T(8,128)(2,1)} %cot_hbm.1, f32[1,128]{1,0:T(1,128)} %gate_hbm.1), custom_call_target="tpu_custom_call" | custom-call | flops 99999997952 | bytes 2097152 | tf_op jit(solution)/shard_map/pack/pallas_call | solution.py:116
  2.8 3.1 %collective-permute-start.11 = (bf16[2,80,512]{2,1,0:T(8,128)(2,1)S(1)}, bf16[2,80,512]{2,1,0:T(8,128)(2,1)S(1)}, u32[]{:S(2)}, u32[]{:S(2)}) collective-permute-start(bf16[2,80,512]{2,1,0:T(8,128)(2,1)S(1)} %get-tuple-element.13.refs_1_), channel_id=1, source_target_pairs={{0,16},{4,12},{8,24},{12,4},{16,0},{20,28},{24,8},{28,20},{1,17},{... | collective-permute-start | bytes 491528 | tf_op jit(solution)/shard_map/ppermute | solution.py:31
  5.8 1.5 %collective-permute-start.12 = (bf16[2,80,512]{2,1,0:T(8,128)(2,1)S(1)}, bf16[2,80,512]{2,1,0:T(8,128)(2,1)S(1)}, u32[]{:S(2)}, u32[]{:S(2)}) collective-permute-start(bf16[2,80,512]{2,1,0:T(8,128)(2,1)S(1)} %get-tuple-element.14.refs_2_), channel_id=1, source_target_pairs={{0,8},{4,20},{8,0},{12,28},{16,24},{20,4},{24,16},{28,12},{1,9},{5... | collective-permute-start | bytes 491528 | tf_op jit(solution)/shard_map/ppermute | solution.py:31
  7.3 0.0 collective-permute-start.13
  7.4 0.0 collective-permute-start.10
  7.4 0.9 %forward.1.small_ref.refs_0_.refs_3_ = bf16[80,1152]{1,0:T(8,128)(2,1)S(1)} custom-call(bf16[2,80,512]{2,1,0:T(8,128)(2,1)S(1)} %get-tuple-element.12.refs_0_, bf16[2,80,512]{2,1,0:T(8,128)(2,1)S(1)} %get-tuple-element.13.refs_1_, bf16[2,80,512]{2,1,0:T(8,128)(2,1)S(1)} %get-tuple-element.14.refs_2_, bf16[2,80,512]{2,1,0:T(8,128)(2,1)S(1)} %get-tuple-element.15.refs_3_, ...), custom_call_target="tpu_custom_call" | custom-call | flops 377487360 | bytes 4718592 | tf_op jit(solution)/shard_map/forward/pallas_call | solution.py:156
  8.3 2.0 %collective-permute-start.4 = (bf16[80,1152]{1,0:T(8,128)(2,1)S(1)}, bf16[80,1152]{1,0:T(8,128)(2,1)S(1)}, u32[]{:S(2)}, u32[]{:S(2)}) collective-permute-start(bf16[80,1152]{1,0:T(8,128)(2,1)S(1)} %forward.1.small_ref.refs_0_.refs_3_), channel_id=1, source_target_pairs={{0,16},{4,12},{8,24},{12,4},{16,0},{20,28},{24,8},{28,20},{1,17},{... | collective-permute-start | bytes 552968 | tf_op jit(solution)/shard_map/ppermute | solution.py:31
  10.3 1.6 %collective-permute-done.11.refs_2_ = bf16[2,80,512]{2,1,0:T(8,128)(2,1)S(1)} collective-permute-done((bf16[2,80,512]{2,1,0:T(8,128)(2,1)S(1)}, bf16[2,80,512]{2,1,0:T(8,128)(2,1)S(1)}, u32[]{:S(2)}, u32[]{:S(2)}) %collective-permute-start.11) | collective-permute-done | bytes 163872 | tf_op jit(solution)/shard_map/ppermute | solution.py:31
  12.0 0.9 %collective-permute-start.5 = (bf16[80,1152]{1,0:T(8,128)(2,1)S(1)}, bf16[80,1152]{1,0:T(8,128)(2,1)S(1)}, u32[]{:S(2)}, u32[]{:S(2)}) collective-permute-start(bf16[80,1152]{1,0:T(8,128)(2,1)S(1)} %forward.1.small_ref.refs_0_.refs_3_), channel_id=1, source_target_pairs={{0,8},{4,20},{8,0},{12,28},{16,24},{20,4},{24,16},{28,12},{1,9},{5... | collective-permute-start | bytes 552968 | tf_op jit(solution)/shard_map/ppermute | solution.py:31
  12.9 0.0 collective-permute-done.12.refs_3_
  12.9 3.4 %collective-permute-start.6 = (bf16[80,1152]{1,0:T(8,128)(2,1)S(1)}, bf16[80,1152]{1,0:T(8,128)(2,1)S(1)}, u32[]{:S(2)}, u32[]{:S(2)}) collective-permute-start(bf16[80,1152]{1,0:T(8,128)(2,1)S(1)} %forward.1.small_ref.refs_0_.refs_3_), channel_id=1, source_target_pairs={{0,24},{4,28},{8,16},{12,20},{16,8},{20,12},{24,0},{28,4},{1,25},{... | collective-permute-start | bytes 552968 | tf_op jit(solution)/shard_map/ppermute | solution.py:31
  16.3 0.0 collective-permute-done.13.refs_4_
  16.3 0.0 collective-permute-start.14
  16.3 0.0 collective-permute-done.10.refs_1_
  16.3 0.5 %collective-permute-start.15 = (bf16[2,80,512]{2,1,0:T(8,128)(2,1)S(1)}, bf16[2,80,512]{2,1,0:T(8,128)(2,1)S(1)}, u32[]{:S(2)}, u32[]{:S(2)}) collective-permute-start(bf16[2,80,512]{2,1,0:T(8,128)(2,1)S(1)} %collective-permute-done.12.refs_3_), channel_id=1, source_target_pairs={{0,4},{4,0},{8,12},{12,8},{16,20},{20,16},{24,28},{28,24},{1,5},{5... | collective-permute-start | bytes 491528 | tf_op jit(solution)/shard_map/ppermute | solution.py:21
  16.8 4.8 %collective-permute-done.4.refs_2_.refs_5_ = bf16[80,1152]{1,0:T(8,128)(2,1)S(1)} collective-permute-done((bf16[80,1152]{1,0:T(8,128)(2,1)S(1)}, bf16[80,1152]{1,0:T(8,128)(2,1)S(1)}, u32[]{:S(2)}, u32[]{:S(2)}) %collective-permute-start.4) | collective-permute-done | bytes 184352 | tf_op jit(solution)/shard_map/ppermute | solution.py:31
  21.6 0.0 collective-permute-start.16
  21.6 0.0 collective-permute-done.5.refs_3_.refs_6_
  21.6 0.5 %collective-permute-start.3 = (bf16[80,1152]{1,0:T(8,128)(2,1)S(1)}, bf16[80,1152]{1,0:T(8,128)(2,1)S(1)}, u32[]{:S(2)}, u32[]{:S(2)}) collective-permute-start(bf16[80,1152]{1,0:T(8,128)(2,1)S(1)} %forward.1.small_ref.refs_0_.refs_3_), channel_id=1, source_target_pairs={{0,4},{4,0},{8,12},{12,8},{16,20},{20,16},{24,28},{28,24},{1,5},{5... | collective-permute-start | bytes 552968 | tf_op jit(solution)/shard_map/ppermute | solution.py:21
  22.1 0.6 %collective-permute-done.6.refs_4_.refs_7_ = bf16[80,1152]{1,0:T(8,128)(2,1)S(1)} collective-permute-done((bf16[80,1152]{1,0:T(8,128)(2,1)S(1)}, bf16[80,1152]{1,0:T(8,128)(2,1)S(1)}, u32[]{:S(2)}, u32[]{:S(2)}) %collective-permute-start.6) | collective-permute-done | bytes 184352 | tf_op jit(solution)/shard_map/ppermute | solution.py:31
  22.7 0.0 collective-permute-start.7
  22.7 0.0 collective-permute-done.14.refs_5_
  22.7 0.5 %collective-permute-start.8 = (bf16[80,1152]{1,0:T(8,128)(2,1)S(1)}, bf16[80,1152]{1,0:T(8,128)(2,1)S(1)}, u32[]{:S(2)}, u32[]{:S(2)}) collective-permute-start(bf16[80,1152]{1,0:T(8,128)(2,1)S(1)} %collective-permute-done.5.refs_3_.refs_6_), channel_id=1, source_target_pairs={{0,4},{4,0},{8,12},{12,8},{16,20},{20,16},{24,28},{28,24},{1,5},{5... | collective-permute-start | bytes 552968 | tf_op jit(solution)/shard_map/ppermute | solution.py:21
  23.2 0.0 collective-permute-done.15.refs_6_
  23.2 0.1 collective-permute-start.9
  23.3 1.2 %back.1 = (bf16[20,2048]{1,0:T(8,128)(2,1)S(1)}, bf16[20,2048]{1,0:T(8,128)(2,1)S(1)}, bf16[20,2048]{1,0:T(8,128)(2,1)S(1)}, bf16[20,2048]{1,0:T(8,128)(2,1)S(1)}) custom-call(bf16[80,1152]{1,0:T(8,128)(2,1)S(1)} %forward.1.small_ref.refs_0_.refs_3_, bf16[1,3,2048,384]{3,2,1,0:T(8,128)(2,1)S(1)} %copy-done), custom_call_target="tpu_custom_call" | custom-call | flops 251658240 | bytes 3145728 | tf_op jit(solution)/shard_map/back/pallas_call | solution.py:199
  24.5 0.0 collective-permute-done.16.refs_7_
  24.5 2.5 %collective-permute-start = (bf16[20,2048]{1,0:T(8,128)(2,1)S(1)}, bf16[20,2048]{1,0:T(8,128)(2,1)S(1)}, u32[]{:S(2)}, u32[]{:S(2)}) collective-permute-start(bf16[20,2048]{1,0:T(8,128)(2,1)S(1)} %get-tuple-element.17), channel_id=1, source_target_pairs={{0,1},{1,0},{2,3},{3,2},{4,5},{5,4},{6,7},{7,6},{8,9},{9,8},{10,11... | collective-permute-start | bytes 245768 | tf_op jit(solution)/shard_map/ppermute | solution.py:21
  27.0 1.2 %tall.1 = (f32[2,640,640]{2,1,0:T(8,128)S(1)}, bf16[2,256,640]{2,1,0:T(8,128)(2,1)S(1)}) custom-call(bf16[2,80,512]{2,1,0:T(8,128)(2,1)S(1)} %get-tuple-element.12.refs_0_, bf16[2,80,512]{2,1,0:T(8,128)(2,1)S(1)} %collective-permute-done.10.refs_1_, bf16[2,80,512]{2,1,0:T(8,128)(2,1)S(1)} %collective-permute-done.11.refs_2_, ...), custom_call_target="tpu_custom_call" | custom-call | flops 838860800 | bytes 5242880 | tf_op jit(solution)/shard_map/tall/pallas_call | solution.py:272
  28.2 0.0 collective-permute-done.3.refs_1_.refs_4_
  28.3 2.6 %collective-permute-start.1 = (bf16[20,2048]{1,0:T(8,128)(2,1)S(1)}, bf16[20,2048]{1,0:T(8,128)(2,1)S(1)}, u32[]{:S(2)}, u32[]{:S(2)}) collective-permute-start(bf16[20,2048]{1,0:T(8,128)(2,1)S(1)} %get-tuple-element.18), channel_id=1, source_target_pairs={{0,2},{1,3},{2,0},{3,1},{4,6},{5,7},{6,4},{7,5},{8,10},{9,11},{10,... | collective-permute-start | bytes 245768 | tf_op jit(solution)/shard_map/ppermute | solution.py:21
  30.9 0.0 collective-permute-done.7.refs_5_.refs_8_
  30.9 0.0 collective-permute-start.2
  30.9 1.2 %first.1.refs_9_ = f32[24,128]{1,0:T(8,128)S(1)} custom-call(bf16[80,1152]{1,0:T(8,128)(2,1)S(1)} %forward.1.small_ref.refs_0_.refs_3_, bf16[80,1152]{1,0:T(8,128)(2,1)S(1)} %collective-permute-done.3.refs_1_.refs_4_, bf16[80,1152]{1,0:T(8,128)(2,1)S(1)} %collective-permute-done.4.refs_2_.refs_5_, ...), custom_call_target="tpu_custom_call" | custom-call | flops 471859200 | bytes 2621440 | tf_op jit(solution)/shard_map/first/pallas_call | solution.py:350
  32.1 0.0 copy-start.2
  32.1 0.0 copy-start.1
  32.2 0.0 collective-permute-done.8.refs_6_.refs_9_
  32.2 0.0 collective-permute-done.9.refs_7_.refs_10_
  32.2 1.2 %last.1 = f32[24,128]{1,0:T(8,128)S(1)} custom-call(bf16[80,1152]{1,0:T(8,128)(2,1)S(1)} %forward.1.small_ref.refs_0_.refs_3_, bf16[80,1152]{1,0:T(8,128)(2,1)S(1)} %collective-permute-done.3.refs_1_.refs_4_, bf16[80,1152]{1,0:T(8,128)(2,1)S(1)} %collective-permute-done.4.refs_2_.refs_5_, bf16[80,1152]{1,0:T(8,128)(2,1)S(1)} %collective-permute-done.5.refs_3_.refs_6_, ...), custom_call_target="tpu_custom_call" | custom-call | flops 235929600 | bytes 2293760 | tf_op jit(solution)/shard_map/last/pallas_call | solution.py:363
  33.4 1.4 %collective-permute-start.17 = (f32[24,128]{1,0:T(8,128)S(1)}, f32[24,128]{1,0:T(8,128)S(1)}, u32[]{:S(2)}, u32[]{:S(2)}) collective-permute-start(f32[24,128]{1,0:T(8,128)S(1)} %last.1), channel_id=1, source_target_pairs={{0,16},{4,20},{8,24},{12,28},{16,0},{20,4},{24,8},{28,12},{1,17},{... | collective-permute-start | bytes 36872 | tf_op jit(solution)/shard_map/ppermute | solution.py:21
  34.8 2.3 %collective-permute-done.17 = f32[24,128]{1,0:T(8,128)S(1)} collective-permute-done((f32[24,128]{1,0:T(8,128)S(1)}, f32[24,128]{1,0:T(8,128)S(1)}, u32[]{:S(2)}, u32[]{:S(2)}) %collective-permute-start.17) | collective-permute-done | bytes 12320 | tf_op jit(solution)/shard_map/ppermute | solution.py:21
  37.2 0.7 %collective-permute-start.18 = (f32[24,128]{1,0:T(8,128)S(1)}, f32[24,128]{1,0:T(8,128)S(1)}, u32[]{:S(2)}, u32[]{:S(2)}) collective-permute-start(f32[24,128]{1,0:T(8,128)S(1)} %add.3.refs_0_), channel_id=1, source_target_pairs={{0,8},{4,12},{8,0},{12,4},{16,24},{20,28},{24,16},{28,20},{1,9},{5... | collective-permute-start | bytes 36872 | tf_op jit(solution)/shard_map/ppermute | solution.py:21
  37.9 0.0 collective-permute-done.refs_1_
  37.9 0.9 %collective-permute-done.1.refs_2_ = bf16[20,2048]{1,0:T(8,128)(2,1)S(1)} collective-permute-done((bf16[20,2048]{1,0:T(8,128)(2,1)S(1)}, bf16[20,2048]{1,0:T(8,128)(2,1)S(1)}, u32[]{:S(2)}, u32[]{:S(2)}) %collective-permute-start.1) | collective-permute-done | bytes 81952 | tf_op jit(solution)/shard_map/ppermute | solution.py:21
  38.7 0.0 collective-permute-done.2.refs_3_
  38.7 0.9 %token_.1 = bf16[1,20,2048]{2,1,0:T(8,128)(2,1)} custom-call(s32[1,4,20]{2,1,0:T(4,128)S(1)} %bitcast.1, bf16[20,2048]{1,0:T(8,128)(2,1)S(1)} %get-tuple-element.16.refs_0_, bf16[20,2048]{1,0:T(8,128)(2,1)S(1)} %collective-permute-done.refs_1_, bf16[20,2048]{1,0:T(8,128)(2,1)S(1)} %collective-permute-done.1.refs_2_, ...), custom_call_target="tpu_custom_call" | custom-call | flops 10485760 | bytes 655360 | tf_op jit(solution)/shard_map/token/pallas_call | solution.py:238
  39.7 1.2 %collective-permute-done.18.refs_1_ = f32[24,128]{1,0:T(8,128)S(1)} collective-permute-done((f32[24,128]{1,0:T(8,128)S(1)}, f32[24,128]{1,0:T(8,128)S(1)}, u32[]{:S(2)}, u32[]{:S(2)}) %collective-permute-start.18) | collective-permute-done | bytes 12320 | tf_op jit(solution)/shard_map/ppermute | solution.py:21
  40.8 2.0 %final.1 = f32[1,3,256,384]{3,2,1,0:T(8,128)} custom-call(f32[24,128]{1,0:T(8,128)S(1)} %add.3.refs_0_, f32[24,128]{1,0:T(8,128)S(1)} %collective-permute-done.18.refs_1_, bf16[2,256,640]{2,1,0:T(8,128)(2,1)S(1)} %get-tuple-element.21.refs_2_, bf16[80,1152]{1,0:T(8,128)(2,1)S(1)} %forward.1.small_ref.refs_0_.refs_3_, ...), custom_call_target="tpu_custom_call" | custom-call | flops 377487360 | bytes 3833856 | tf_op jit(solution)/shard_map/final/pallas_call | solution.py:427
  (5 shorter events, 0.0 us)
Async XLA Ops:
  0.6 6.8 %copy-start = (bf16[1,3,2048,384]{3,2,1,0:T(8,128)(2,1)S(1)}, bf16[1,3,2048,384]{3,2,1,0:T(8,128)(2,1)}, u32[]{:S(2)}) copy-start(bf16[1,3,2048,384]{3,2,1,0:T(8,128)(2,1)} %w_ref.1) | copy-start | bytes 14155780
  2.8 9.2 %collective-permute-start.11 = (bf16[2,80,512]{2,1,0:T(8,128)(2,1)S(1)}, bf16[2,80,512]{2,1,0:T(8,128)(2,1)S(1)}, u32[]{:S(2)}, u32[]{:S(2)}) collective-permute-start(bf16[2,80,512]{2,1,0:T(8,128)(2,1)S(1)} %get-tuple-element.13.refs_1_), channel_id=1, source_target_pairs={{0,16},{4,12},{8,24},{12,4},{16,0},{20,28},{24,8},{28,20},{1,17},{... | collective-permute-start | bytes 491528 | tf_op jit(solution)/shard_map/ppermute | solution.py:31
  5.8 7.1 %collective-permute-start.12 = (bf16[2,80,512]{2,1,0:T(8,128)(2,1)S(1)}, bf16[2,80,512]{2,1,0:T(8,128)(2,1)S(1)}, u32[]{:S(2)}, u32[]{:S(2)}) collective-permute-start(bf16[2,80,512]{2,1,0:T(8,128)(2,1)S(1)} %get-tuple-element.14.refs_2_), channel_id=1, source_target_pairs={{0,8},{4,20},{8,0},{12,28},{16,24},{20,4},{24,16},{28,12},{1,9},{5... | collective-permute-start | bytes 491528 | tf_op jit(solution)/shard_map/ppermute | solution.py:31
  7.3 8.9 %collective-permute-start.13 = (bf16[2,80,512]{2,1,0:T(8,128)(2,1)S(1)}, bf16[2,80,512]{2,1,0:T(8,128)(2,1)S(1)}, u32[]{:S(2)}, u32[]{:S(2)}) collective-permute-start(bf16[2,80,512]{2,1,0:T(8,128)(2,1)S(1)} %get-tuple-element.15.refs_3_), channel_id=1, source_target_pairs={{0,24},{4,28},{8,16},{12,20},{16,8},{20,12},{24,0},{28,4},{1,25},{... | collective-permute-start | bytes 491528 | tf_op jit(solution)/shard_map/ppermute | solution.py:31
  7.4 8.9 %collective-permute-start.10 = (bf16[2,80,512]{2,1,0:T(8,128)(2,1)S(1)}, bf16[2,80,512]{2,1,0:T(8,128)(2,1)S(1)}, u32[]{:S(2)}, u32[]{:S(2)}) collective-permute-start(bf16[2,80,512]{2,1,0:T(8,128)(2,1)S(1)} %get-tuple-element.12.refs_0_), channel_id=1, source_target_pairs={{0,4},{4,0},{8,12},{12,8},{16,20},{20,16},{24,28},{28,24},{1,5},{5... | collective-permute-start | bytes 491528 | tf_op jit(solution)/shard_map/ppermute | solution.py:21
  8.3 13.3 %collective-permute-start.4 = (bf16[80,1152]{1,0:T(8,128)(2,1)S(1)}, bf16[80,1152]{1,0:T(8,128)(2,1)S(1)}, u32[]{:S(2)}, u32[]{:S(2)}) collective-permute-start(bf16[80,1152]{1,0:T(8,128)(2,1)S(1)} %forward.1.small_ref.refs_0_.refs_3_), channel_id=1, source_target_pairs={{0,16},{4,12},{8,24},{12,4},{16,0},{20,28},{24,8},{28,20},{1,17},{... | collective-permute-start | bytes 552968 | tf_op jit(solution)/shard_map/ppermute | solution.py:31
  12.0 9.7 %collective-permute-start.5 = (bf16[80,1152]{1,0:T(8,128)(2,1)S(1)}, bf16[80,1152]{1,0:T(8,128)(2,1)S(1)}, u32[]{:S(2)}, u32[]{:S(2)}) collective-permute-start(bf16[80,1152]{1,0:T(8,128)(2,1)S(1)} %forward.1.small_ref.refs_0_.refs_3_), channel_id=1, source_target_pairs={{0,8},{4,20},{8,0},{12,28},{16,24},{20,4},{24,16},{28,12},{1,9},{5... | collective-permute-start | bytes 552968 | tf_op jit(solution)/shard_map/ppermute | solution.py:31
  12.9 9.8 %collective-permute-start.6 = (bf16[80,1152]{1,0:T(8,128)(2,1)S(1)}, bf16[80,1152]{1,0:T(8,128)(2,1)S(1)}, u32[]{:S(2)}, u32[]{:S(2)}) collective-permute-start(bf16[80,1152]{1,0:T(8,128)(2,1)S(1)} %forward.1.small_ref.refs_0_.refs_3_), channel_id=1, source_target_pairs={{0,24},{4,28},{8,16},{12,20},{16,8},{20,12},{24,0},{28,4},{1,25},{... | collective-permute-start | bytes 552968 | tf_op jit(solution)/shard_map/ppermute | solution.py:31
  16.3 6.5 %collective-permute-start.14 = (bf16[2,80,512]{2,1,0:T(8,128)(2,1)S(1)}, bf16[2,80,512]{2,1,0:T(8,128)(2,1)S(1)}, u32[]{:S(2)}, u32[]{:S(2)}) collective-permute-start(bf16[2,80,512]{2,1,0:T(8,128)(2,1)S(1)} %collective-permute-done.11.refs_2_), channel_id=1, source_target_pairs={{0,4},{4,0},{8,12},{12,8},{16,20},{20,16},{24,28},{28,24},{1,5},{5... | collective-permute-start | bytes 491528 | tf_op jit(solution)/shard_map/ppermute | solution.py:21
  16.3 7.0 %collective-permute-start.15 = (bf16[2,80,512]{2,1,0:T(8,128)(2,1)S(1)}, bf16[2,80,512]{2,1,0:T(8,128)(2,1)S(1)}, u32[]{:S(2)}, u32[]{:S(2)}) collective-permute-start(bf16[2,80,512]{2,1,0:T(8,128)(2,1)S(1)} %collective-permute-done.12.refs_3_), channel_id=1, source_target_pairs={{0,4},{4,0},{8,12},{12,8},{16,20},{20,16},{24,28},{28,24},{1,5},{5... | collective-permute-start | bytes 491528 | tf_op jit(solution)/shard_map/ppermute | solution.py:21
  21.6 2.9 %collective-permute-start.16 = (bf16[2,80,512]{2,1,0:T(8,128)(2,1)S(1)}, bf16[2,80,512]{2,1,0:T(8,128)(2,1)S(1)}, u32[]{:S(2)}, u32[]{:S(2)}) collective-permute-start(bf16[2,80,512]{2,1,0:T(8,128)(2,1)S(1)} %collective-permute-done.13.refs_4_), channel_id=1, source_target_pairs={{0,4},{4,0},{8,12},{12,8},{16,20},{20,16},{24,28},{28,24},{1,5},{5... | collective-permute-start | bytes 491528 | tf_op jit(solution)/shard_map/ppermute | solution.py:21
  21.6 6.6 %collective-permute-start.3 = (bf16[80,1152]{1,0:T(8,128)(2,1)S(1)}, bf16[80,1152]{1,0:T(8,128)(2,1)S(1)}, u32[]{:S(2)}, u32[]{:S(2)}) collective-permute-start(bf16[80,1152]{1,0:T(8,128)(2,1)S(1)} %forward.1.small_ref.refs_0_.refs_3_), channel_id=1, source_target_pairs={{0,4},{4,0},{8,12},{12,8},{16,20},{20,16},{24,28},{28,24},{1,5},{5... | collective-permute-start | bytes 552968 | tf_op jit(solution)/shard_map/ppermute | solution.py:21
  22.7 8.2 %collective-permute-start.7 = (bf16[80,1152]{1,0:T(8,128)(2,1)S(1)}, bf16[80,1152]{1,0:T(8,128)(2,1)S(1)}, u32[]{:S(2)}, u32[]{:S(2)}) collective-permute-start(bf16[80,1152]{1,0:T(8,128)(2,1)S(1)} %collective-permute-done.4.refs_2_.refs_5_), channel_id=1, source_target_pairs={{0,4},{4,0},{8,12},{12,8},{16,20},{20,16},{24,28},{28,24},{1,5},{5... | collective-permute-start | bytes 552968 | tf_op jit(solution)/shard_map/ppermute | solution.py:21
  22.7 9.4 %collective-permute-start.8 = (bf16[80,1152]{1,0:T(8,128)(2,1)S(1)}, bf16[80,1152]{1,0:T(8,128)(2,1)S(1)}, u32[]{:S(2)}, u32[]{:S(2)}) collective-permute-start(bf16[80,1152]{1,0:T(8,128)(2,1)S(1)} %collective-permute-done.5.refs_3_.refs_6_), channel_id=1, source_target_pairs={{0,4},{4,0},{8,12},{12,8},{16,20},{20,16},{24,28},{28,24},{1,5},{5... | collective-permute-start | bytes 552968 | tf_op jit(solution)/shard_map/ppermute | solution.py:21
  23.2 8.9 %collective-permute-start.9 = (bf16[80,1152]{1,0:T(8,128)(2,1)S(1)}, bf16[80,1152]{1,0:T(8,128)(2,1)S(1)}, u32[]{:S(2)}, u32[]{:S(2)}) collective-permute-start(bf16[80,1152]{1,0:T(8,128)(2,1)S(1)} %collective-permute-done.6.refs_4_.refs_7_), channel_id=1, source_target_pairs={{0,4},{4,0},{8,12},{12,8},{16,20},{20,16},{24,28},{28,24},{1,5},{5... | collective-permute-start | bytes 552968 | tf_op jit(solution)/shard_map/ppermute | solution.py:21
  24.5 13.4 %collective-permute-start = (bf16[20,2048]{1,0:T(8,128)(2,1)S(1)}, bf16[20,2048]{1,0:T(8,128)(2,1)S(1)}, u32[]{:S(2)}, u32[]{:S(2)}) collective-permute-start(bf16[20,2048]{1,0:T(8,128)(2,1)S(1)} %get-tuple-element.17), channel_id=1, source_target_pairs={{0,1},{1,0},{2,3},{3,2},{4,5},{5,4},{6,7},{7,6},{8,9},{9,8},{10,11... | collective-permute-start | bytes 245768 | tf_op jit(solution)/shard_map/ppermute | solution.py:21
  28.3 10.5 %collective-permute-start.1 = (bf16[20,2048]{1,0:T(8,128)(2,1)S(1)}, bf16[20,2048]{1,0:T(8,128)(2,1)S(1)}, u32[]{:S(2)}, u32[]{:S(2)}) collective-permute-start(bf16[20,2048]{1,0:T(8,128)(2,1)S(1)} %get-tuple-element.18), channel_id=1, source_target_pairs={{0,2},{1,3},{2,0},{3,1},{4,6},{5,7},{6,4},{7,5},{8,10},{9,11},{10,... | collective-permute-start | bytes 245768 | tf_op jit(solution)/shard_map/ppermute | solution.py:21
  30.9 7.8 %collective-permute-start.2 = (bf16[20,2048]{1,0:T(8,128)(2,1)S(1)}, bf16[20,2048]{1,0:T(8,128)(2,1)S(1)}, u32[]{:S(2)}, u32[]{:S(2)}) collective-permute-start(bf16[20,2048]{1,0:T(8,128)(2,1)S(1)} %get-tuple-element.19), channel_id=1, source_target_pairs={{0,3},{1,2},{2,1},{3,0},{4,7},{5,6},{6,5},{7,4},{8,11},{9,10},{10,... | collective-permute-start | bytes 245768 | tf_op jit(solution)/shard_map/ppermute | solution.py:21
  32.1 6.6 %copy-start.2 = (s32[1,20,4]{1,2,0:T(4,128)S(1)}, s32[1,20,4]{1,2,0:T(4,128)}, u32[]{:S(2)}) copy-start(s32[1,20,4]{1,2,0:T(4,128)} %param.9) | copy-start | bytes 964
  32.1 8.7 %copy-start.1 = (f32[1,3,256,384]{3,2,1,0:T(8,128)S(1)}, f32[1,3,256,384]{3,2,1,0:T(8,128)}, u32[]{:S(2)}) copy-start(f32[1,3,256,384]{3,2,1,0:T(8,128)} %refs_11_.1) | copy-start | bytes 3538948
  33.4 3.8 %collective-permute-start.17 = (f32[24,128]{1,0:T(8,128)S(1)}, f32[24,128]{1,0:T(8,128)S(1)}, u32[]{:S(2)}, u32[]{:S(2)}) collective-permute-start(f32[24,128]{1,0:T(8,128)S(1)} %last.1), channel_id=1, source_target_pairs={{0,16},{4,20},{8,24},{12,28},{16,0},{20,4},{24,8},{28,12},{1,17},{... | collective-permute-start | bytes 36872 | tf_op jit(solution)/shard_map/ppermute | solution.py:21
  37.2 3.7 %collective-permute-start.18 = (f32[24,128]{1,0:T(8,128)S(1)}, f32[24,128]{1,0:T(8,128)S(1)}, u32[]{:S(2)}, u32[]{:S(2)}) collective-permute-start(f32[24,128]{1,0:T(8,128)S(1)} %add.3.refs_0_), channel_id=1, source_target_pairs={{0,8},{4,12},{8,0},{12,4},{16,24},{20,28},{24,16},{28,20},{1,9},{5... | collective-permute-start | bytes 36872 | tf_op jit(solution)/shard_map/ppermute | solution.py:21

commit v2 on v1

--- a/solution.py
+++ b/solution.py
@@ -77,60 +77,86 @@
     return place
 
 
-def pack_kernel(sizes, x_hbm, cot_hbm, gate_hbm, *refs):
-    owners, cap, live, chips, width, _ = sizes
-    out_refs, (x_ref, cot_ref, gate_ref, sems, gate_sem) = refs[:chips], refs[chips:]
+def turn_columns(turn, width):
+    me = lax.axis_index("rep")
+    chip = (me >> 1) ^ turn_step(me & 1, turn)
+    return pl.ds(pl.multiple_of(chip * 2 * width, 2 * width), 2 * width)
+
+
+def pack(sizes, x, cot, gate, out_ref):
+    owners, cap, live, _, width, _ = sizes
     slots, rows = owners * cap, owners * live
-    me = lax.axis_index("rep")
-    gate_copy = pltpu.make_async_copy(gate_hbm, gate_ref, gate_sem)
-    gate_copy.start()
-    copies = []
-    for k in range(chips):
-        chip = (me >> 1) ^ turn_step(me & 1, k)
-        at = pl.ds(pl.multiple_of(chip * 2 * width, 2 * width), 2 * width)
-        for side, (source, target) in enumerate([(x_hbm, x_ref), (cot_hbm, cot_ref)]):
-            copy = pltpu.make_async_copy(source.at[0, :, at], target.at[k], sems.at[k, side])
-            copy.start()
-            copies.append(copy)
     place = spread_rows(lax.broadcasted_iota(jnp.int32, (rows, slots), 0), live, cap, owners)
     slot = lax.broadcasted_iota(jnp.int32, (rows, slots), 1)
     select = jnp.where(place == slot, 1.0, 0.0).astype(bf16)
     line = lax.broadcasted_iota(jnp.int32, (slots, slots), 0)
     lane = lax.broadcasted_iota(jnp.int32, (slots, slots), 1)
-    gate_copy.wait()
-    gate = jnp.sum(jnp.where(line == lane, gate_ref[...], 0.0), axis=1, keepdims=True)
-    for k in range(chips):
-        copies[2 * k].wait()
-        copies[2 * k + 1].wait()
-        scaled = (gate * cot_ref[k].astype(f32)).astype(bf16)
-        routed = jnp.dot(select, x_ref[k], preferred_element_type=f32).astype(bf16)
-        scaled = jnp.dot(select, scaled, preferred_element_type=f32).astype(bf16)
-        for core in range(2):
-            out_refs[k][core, :, :width] = routed[:, core * width : (core + 1) * width]
-            out_refs[k][core, :, width:] = scaled[:, core * width : (core + 1) * width]
-
-
-def pack_call(x_rows, row_cot, gate_vals, sizes):
+    gate = jnp.sum(jnp.where(line == lane, gate, 0.0), axis=1, keepdims=True)
+    scaled = (gate * cot.astype(f32)).astype(bf16)
+    routed = jnp.dot(select, x, preferred_element_type=f32).astype(bf16)
+    scaled = jnp.dot(select, scaled, preferred_element_type=f32).astype(bf16)
+    for core in range(2):
+        out_ref[core, :, :width] = routed[:, core * width : (core + 1) * width]
+        out_ref[core, :, width:] = scaled[:, core * width : (core + 1) * width]
+
+
+def pack_one_kernel(sizes, x_hbm, cot_hbm, gate_hbm, out_ref, x_ref, cot_ref, gate_ref, sems):
+    at = turn_columns(1, sizes[4])
+    copies = [
+        pltpu.make_async_copy(x_hbm.at[0, :, at], x_ref, sems.at[0]),
+        pltpu.make_async_copy(cot_hbm.at[0, :, at], cot_ref, sems.at[1]),
+        pltpu.make_async_copy(gate_hbm, gate_ref, sems.at[2]),
+    ]
+    for copy in copies:
+        copy.start()
+    for copy in copies:
+        copy.wait()
+    pack(sizes, x_ref[...], cot_ref[...], gate_ref[...], out_ref)
+
+
+def pack_rest_kernel(sizes, turns, x_ref, cot_ref, gate_ref, *out_refs):
+    for turn, out_ref in zip(turns, out_refs, strict=True):
+        at = turn_columns(turn, sizes[4])
+        pack(sizes, x_ref[0, :, at], cot_ref[0, :, at], gate_ref[...], out_ref)
+
+
+def pack_one_call(x_rows, row_cot, gate_vals, sizes):
     owners, cap, live, chips, width, _ = sizes
-    rows = owners * live
-    return pl.pallas_call(
-        functools.partial(pack_kernel, sizes),
-        out_shape=[jax.ShapeDtypeStruct((2, rows, 2 * width), bf16)] * chips,
+    block = pltpu.VMEM((owners * cap, 2 * width), bf16)
+    return pl.pallas_call(
+        functools.partial(pack_one_kernel, sizes),
+        out_shape=jax.ShapeDtypeStruct((2, owners * live, 2 * width), bf16),
         in_specs=[HBM] * 3,
-        out_specs=[VMEM] * chips,
+        out_specs=VMEM,
         scratch_shapes=[
-            pltpu.VMEM((chips, owners * cap, 2 * width), bf16),
-            pltpu.VMEM((chips, owners * cap, 2 * width), bf16),
+            block,
+            block,
             pltpu.VMEM((1, owners * cap), f32),
-            pltpu.SemaphoreType.DMA((chips, 2)),
-            pltpu.SemaphoreType.DMA,
+            pltpu.SemaphoreType.DMA((3,)),
         ],
-        compiler_params=kernel_params(6),
-        cost_estimate=pl.CostEstimate(
-            flops=pack_flops, bytes_accessed=8 * x_rows.size, transcendentals=0
-        ),
-        name="pack",
+        compiler_params=kernel_params(4),
+        cost_estimate=pl.CostEstimate(
+            flops=pack_flops, bytes_accessed=8 * x_rows.size // chips, transcendentals=0
+        ),
+        name="pack_one",
     )(in_hbm(x_rows), in_hbm(row_cot), in_hbm(gate_vals))
+
+
+def pack_rest_call(x_rows, row_cot, gate_vals, sizes):
+    owners, _, live, chips, width, _ = sizes
+    turns = [k for k in range(chips) if k != 1]
+    shape = jax.ShapeDtypeStruct((2, owners * live, 2 * width), bf16)
+    return pl.pallas_call(
+        functools.partial(pack_rest_kernel, sizes, turns),
+        out_shape=[shape] * len(turns),
+        in_specs=[VMEM] * 3,
+        out_specs=[VMEM] * len(turns),
+        compiler_params=kernel_params(4),
+        cost_estimate=pl.CostEstimate(
+            flops=4 * owners * live * x_rows.size, bytes_accessed=8 * x_rows.size, transcendentals=0
+        ),
+        name="pack_rest",
+    )(x_rows, row_cot, gate_vals)
 
 
 def forward_kernel(sizes, *refs):
@@ -251,39 +277,40 @@
     )(route_pos.swapaxes(1, 2), *returned)
 
 
-def tall_kernel(reps, *refs):
-    tall_refs, gram_ref, flip_ref = refs[:reps], refs[reps], refs[reps + 1]
-    width = tall_refs[0].shape[2] // 2
+def tall_kernel(start, *refs):
+    tall_refs, gram_ref, flip_ref = refs[:-2], refs[-2], refs[-1]
+    rows, width = tall_refs[0].shape[1], tall_refs[0].shape[2] // 2
     core = lax.axis_index("rep") & 1
     for side in range(2):
         at = slice(side * width, (side + 1) * width)
         both = jnp.concatenate(
             [jnp.concatenate([ref[0, :, at], ref[1, :, at]], axis=1) for ref in tall_refs], axis=0
         )
-        gram_ref[side] = lax.dot_general(both, both, contract_cols, preferred_element_type=f32)
-        own = jnp.concatenate([ref[core, :, at] for ref in tall_refs], axis=0)
+        gram_ref[side] = lax.dot_general(
+            both[start * rows :], both, contract_cols, preferred_element_type=f32
+        )
+        own = jnp.concatenate([ref[core, :, at] for ref in tall_refs[start:]], axis=0)
         flip_ref[side] = own.T
 
 
-def tall_call(tall):
-    reps, (cores, rows, width) = len(tall), tall[0].shape
+def tall_call(tall, start):
+    blocks, (cores, rows, width) = len(tall), tall[0].shape
     width //= 2
-    flat = reps * rows
-    return pl.pallas_call(
-        functools.partial(tall_kernel, reps),
+    flat, most = blocks * rows, (blocks - start) * rows
+    return pl.pallas_call(
+        functools.partial(tall_kernel, start),
         out_shape=[
-            jax.ShapeDtypeStruct((2, flat, flat), f32),
-            jax.ShapeDtypeStruct((2, width, flat), bf16),
+            jax.ShapeDtypeStruct((2, most, flat), f32),
+            jax.ShapeDtypeStruct((2, width, most), bf16),
         ],
-        in_specs=[VMEM] * reps,
+        in_specs=[VMEM] * blocks,
         out_specs=[VMEM] * 2,
         compiler_params=kernel_params(6),
         cost_estimate=pl.CostEstimate(
-            flops=8 * flat * flat * width,
-            bytes_accessed=8 * flat * flat + 12 * flat * width,
+            flops=8 * flat * most * width,
+            bytes_accessed=8 * flat * most + 12 * flat * width,
             transcendentals=0,
         ),
-        name="tall",
     )(*tall)
 
 
@@ -302,7 +329,7 @@
         both = lax.dot_general(
             block[start * rows :], block, contract_cols, preferred_element_type=f32
         )
-        both = both * tall_ref[t // 2, start * rows : flat, :flat]
+        both = both * tall_ref[t // 2]
         both = both.reshape(reps - start, rows // 8, 8, flat)
         sums.append(jnp.sum(both, axis=1).reshape((reps - start) * 8, flat))
     sums = jnp.dot(
@@ -343,7 +370,7 @@
         out_ref[t * reps : (t + 1) * reps, :] = gram
 
 
-def gram_calls(wide, tall_gram, ff):
+def gram_calls(wide, first_tall, last_tall, ff):
     reps, rows = len(wide), wide[0].shape[0]
     flat = reps * rows
     shape = jax.ShapeDtypeStruct((3 * reps, 128), f32)
@@ -359,7 +386,7 @@
             transcendentals=0,
         ),
         name="first",
-    )(*wide[:-late_blocks], tall_gram)
+    )(*wide[:-late_blocks], first_tall)
     return pl.pallas_call(
         functools.partial(last_kernel, reps, ff),
         out_shape=shape,
@@ -372,11 +399,11 @@
             transcendentals=0,
         ),
         name="last",
-    )(*wide, tall_gram, first)
+    )(*wide, last_tall, first)
 
 
 def final_kernel(reps, ff, *refs):
-    gram_refs, flip_ref, refs = refs[:2], refs[2], refs[3:]
+    gram_refs, flip_refs, refs = refs[:2], refs[2:4], refs[4:]
     wide_refs, (moment_ref, out_hbm, coef_ref, out_ref, sems) = refs[:reps], refs[reps:]
     copies = []
     me = lax.axis_index("rep")
@@ -412,9 +439,10 @@
         for k in range(reps):
             coef = coef_ref[pl.ds(t * reps + replica_of(me, k), 1), :]
             scaled.append((coef * wide_refs[k][:, t * ff : (t + 1) * ff].astype(f32)).astype(bf16))
-        combined = jnp.dot(
-            flip_ref[t // 2], jnp.concatenate(scaled, axis=0), preferred_element_type=f32
-        )
+        combined = 0.0
+        for flip_ref, part in zip(flip_refs, (scaled[:-late_blocks], scaled[-late_blocks:])):
+            part = jnp.concatenate(part, axis=0)
+            combined += jnp.dot(flip_ref[t // 2], part, preferred_element_type=f32)
         out_ref[0, t] = moment_decay * moment_ref[0, t] + (1.0 - moment_decay) * combined
         copies.append(pltpu.make_async_copy(out_ref.at[0, t], out_hbm.at[0, t], sems.at[t]))
         copies[t].start()
@@ -422,12 +450,12 @@
         copy.wait()
 
 
-def final_call(grams, flip, wide, momentum, ff):
+def final_call(grams, flips, wide, momentum, ff):
     reps, rows = len(wide), wide[0].shape[0]
     return pl.pallas_call(
         functools.partial(final_kernel, reps, ff),
         out_shape=jax.ShapeDtypeStruct(momentum.shape, f32),
-        in_specs=[VMEM] * (len(grams) + reps + 2),
+        in_specs=[VMEM] * (len(grams) + len(flips) + reps + 1),
         out_specs=HBM,
         scratch_shapes=[
             pltpu.VMEM((3 * reps, ff), f32),
@@ -441,7 +469,7 @@
             transcendentals=0,
         ),
         name="final",
-    )(*grams, flip, *wide, momentum)
+    )(*grams, *flips, *wide, momentum)
 
 
 def adasum_weights(gram):
@@ -534,7 +562,9 @@
 
 def with_kernels(x_rows, row_cot, gate_vals, route_pos, weights, momentum, sizes):
     owners, cap, _, chips, _, ff = sizes
-    pairs = pack_call(x_rows, row_cot, gate_vals, sizes)
+    pair = pack_one_call(x_rows, row_cot, gate_vals, sizes)
+    pairs = pack_rest_call(x_rows, row_cot, gate_vals, sizes)
+    pairs = [pairs[0], pair, *pairs[1:]]
     tall = turns(pairs)
     small = forward_call(pairs, weights, sizes)
     wide = turns([small] * chips)
@@ -543,11 +573,13 @@
         returned[k] = swap(returned[k], "exp", k)
     token_grad = token_call(route_pos, returned, cap)
     tall, wide = core_swaps(tall), core_swaps(wide)
-    tall_gram, flip = tall_call(tall)
-    gram = gram_calls(wide, tall_gram, ff)
+    start = len(tall) - late_blocks
+    first_tall, first_flip = tall_call(tall[:start], 0)
+    last_tall, last_flip = tall_call(tall, start)
+    gram = gram_calls(wide, first_tall, last_tall, ff)
     gram = gram + swap(gram, "rep", 4)
     grams = [gram, swap(gram, "rep", 2)]
-    return token_grad, final_call(grams, flip, wide, momentum, ff)
+    return token_grad, final_call(grams, [first_flip, last_flip], wide, momentum, ff)
 
 
 def without_kernels(x_rows, row_cot, gate_vals, route_pos, weights, momentum, sizes):

time: 43 us -> 44.4 us (1.033)
  starting transfers between devices: 19.8 us -> 15.7 us
  local copies, waits for them, and re-layouts: 0.02 us -> 3.71 us
  waiting for transfers between devices: 11.5 us -> 13.6 us
    unnamed x6 -> x12, local copies, waits for them, and re-layouts: 0.02 us -> 3.71 us
    ppermute x6, starting transfers between devices: 10.9 us -> 7.71 us  [turn_swap(): return lax.ppermute(block, 'rep', route)]
    ppermute x6, waiting for transfers between devices: 7.11 us -> 8.91 us  [turn_swap(): return lax.ppermute(block, 'rep', route)]
    ppermute x13, starting transfers between devices: 8.95 us -> 7.99 us  [swap(): return lax.ppermute(block, axis, [(i, i ^ mask) for i in range(count)])]
    pallas_call x2 -> x4, Pallas kernels: 3.34 us -> 2.92 us  [the longest x1 1.39 us: pack_one_call(): pl.pallas_call(functools.partial(pack_one_kernel, sizes), out_shape=jax.S...]
  transfers between devices with their start and end apart: 19 -> 19, of which waited for: 6 -> 6; matrix products, arithmetic and copies ran while one was open for 0% -> 0% of each run, Pallas kernels for 16% -> 18%
where the time goes in v2:
time: 44.4 us; the launch traced here: 44.2 us
  starting transfers between devices  15.7 us (35%)
  waiting for transfers between devices  13.6 us (31%)
  Pallas kernels  10.4 us (23%)
  local copies, waits for them, and re-layouts  3.71 us (8%)
  between operations  0.76 us (2%)
    ppermute x6, waiting for transfers between devices, turn_swap(): return lax.ppermute(block, 'rep', route)  8.91 us
    ppermute x13, starting transfers between devices, swap(): return lax.ppermute(block, axis, [(i, i ^ mask) for i in range(count)])  7.99 us
    ppermute x6, starting transfers between devices, turn_swap(): return lax.ppermute(block, 'rep', route)  7.71 us
    ppermute x13, waiting for transfers between devices, swap(): return lax.ppermute(block, axis, [(i, i ^ mask) for i in range(count)])  4.71 us
    unnamed x12, local copies, waits for them, and re-layouts  3.71 us
    pallas_call x1, Pallas kernels, final_call(): pl.pallas_call(functools.partial(final_kernel, reps, ff), out_shape=jax.S...  2.05 us
    pallas_call x1, Pallas kernels, pack_one_call(): pl.pallas_call(functools.partial(pack_one_kernel, sizes), out_shape=jax.S...  1.39 us
    pallas_call x1, Pallas kernels, gram_calls(): pl.pallas_call(functools.partial(first_kernel, reps, ff), out_shape=shape...  1.21 us
  transfers between devices with their start and end apart: 19, of which 6 were waited for; matrix products, arithmetic and copies ran while one was open for 0% of the time, Pallas kernels for 18%

profile of v2, /device:TPU:0, one launch (start us, length us, event | category | flops | bytes accessed | tf_op | source)
XLA Modules:
  0.0 44.2 jit_solution(8495414728390113519)
XLA Ops:
  0.6 0.0 copy-start.2
  0.6 1.0 %copy-done.2 = bf16[1,128,2048]{2,1,0:T(8,128)(2,1)S(1)} copy-done((bf16[1,128,2048]{2,1,0:T(8,128)(2,1)S(1)}, bf16[1,128,2048]{2,1,0:T(8,128)(2,1)}, u32[]{:S(2)}) %copy-start.2) | copy-done | bytes 524312
  1.7 1.0 %copy-done.3 = bf16[1,128,2048]{2,1,0:T(8,128)(2,1)S(1)} copy-done((bf16[1,128,2048]{2,1,0:T(8,128)(2,1)S(1)}, bf16[1,128,2048]{2,1,0:T(8,128)(2,1)}, u32[]{:S(2)}) %copy-start.3) | copy-done | bytes 524312
  2.7 0.7 %copy-done.5 = f32[1,128]{1,0:T(1,128)S(1)} copy-done((f32[1,128]{1,0:T(1,128)S(1)}, f32[1,128]{1,0:T(1,128)}, u32[]{:S(2)}) %copy-start.5) | copy-done | bytes 536
  3.4 0.3 pack_rest.1
  3.7 0.6 %collective-permute-start.10 = (bf16[2,80,512]{2,1,0:T(8,128)(2,1)S(1)}, bf16[2,80,512]{2,1,0:T(8,128)(2,1)S(1)}, u32[]{:S(2)}, u32[]{:S(2)}) collective-permute-start(bf16[2,80,512]{2,1,0:T(8,128)(2,1)S(1)} %get-tuple-element.13.refs_0_), channel_id=1, source_target_pairs={{0,4},{4,0},{8,12},{12,8},{16,20},{20,16},{24,28},{28,24},{1,5},{5... | collective-permute-start | bytes 491528 | tf_op jit(solution)/shard_map/ppermute | solution.py:21
  4.3 2.6 %collective-permute-start.12 = (bf16[2,80,512]{2,1,0:T(8,128)(2,1)S(1)}, bf16[2,80,512]{2,1,0:T(8,128)(2,1)S(1)}, u32[]{:S(2)}, u32[]{:S(2)}) collective-permute-start(bf16[2,80,512]{2,1,0:T(8,128)(2,1)S(1)} %get-tuple-element.14.refs_2_), channel_id=1, source_target_pairs={{0,8},{4,20},{8,0},{12,28},{16,24},{20,4},{24,16},{28,12},{1,9},{5... | collective-permute-start | bytes 491528 | tf_op jit(solution)/shard_map/ppermute | solution.py:31
  6.8 1.5 %collective-permute-start.13 = (bf16[2,80,512]{2,1,0:T(8,128)(2,1)S(1)}, bf16[2,80,512]{2,1,0:T(8,128)(2,1)S(1)}, u32[]{:S(2)}, u32[]{:S(2)}) collective-permute-start(bf16[2,80,512]{2,1,0:T(8,128)(2,1)S(1)} %get-tuple-element.15.refs_3_), channel_id=1, source_target_pairs={{0,24},{4,28},{8,16},{12,20},{16,8},{20,12},{24,0},{28,4},{1,25},{... | collective-permute-start | bytes 491528 | tf_op jit(solution)/shard_map/ppermute | solution.py:31
  8.3 1.4 %pack_one.1.refs_1_ = bf16[2,80,512]{2,1,0:T(8,128)(2,1)S(1)} custom-call(bf16[1,128,2048]{2,1,0:T(8,128)(2,1)} %x_hbm.1, bf16[1,128,2048]{2,1,0:T(8,128)(2,1)} %cot_hbm.1, f32[1,128]{1,0:T(1,128)} %gate_hbm.1), custom_call_target="tpu_custom_call" | custom-call | flops 99999997952 | bytes 524288 | tf_op jit(solution)/shard_map/pack_one/pallas_call | solution.py:126
  9.7 0.1 collective-permute-start.11
  9.8 1.0 %copy-done = bf16[1,3,2048,384]{3,2,1,0:T(8,128)(2,1)S(1)} copy-done((bf16[1,3,2048,384]{3,2,1,0:T(8,128)(2,1)S(1)}, bf16[1,3,2048,384]{3,2,1,0:T(8,128)(2,1)}, u32[]{:S(2)}) %copy-start) | copy-done | bytes 4718616
  10.8 0.9 %forward.1.small_ref.refs_0_.refs_4_ = bf16[80,1152]{1,0:T(8,128)(2,1)S(1)} custom-call(bf16[2,80,512]{2,1,0:T(8,128)(2,1)S(1)} %get-tuple-element.13.refs_0_, bf16[2,80,512]{2,1,0:T(8,128)(2,1)S(1)} %pack_one.1.refs_1_, bf16[2,80,512]{2,1,0:T(8,128)(2,1)S(1)} %get-tuple-element.14.refs_2_, bf16[2,80,512]{2,1,0:T(8,128)(2,1)S(1)} %get-tuple-element.15.refs_3_, ...), custom_call_target="tpu_custom_call" | custom-call | flops 377487360 | bytes 4718592 | tf_op jit(solution)/shard_map/forward/pallas_call | solution.py:182
  11.7 1.1 %collective-permute-start.4 = (bf16[80,1152]{1,0:T(8,128)(2,1)S(1)}, bf16[80,1152]{1,0:T(8,128)(2,1)S(1)}, u32[]{:S(2)}, u32[]{:S(2)}) collective-permute-start(bf16[80,1152]{1,0:T(8,128)(2,1)S(1)} %forward.1.small_ref.refs_0_.refs_4_), channel_id=1, source_target_pairs={{0,16},{4,12},{8,24},{12,4},{16,0},{20,28},{24,8},{28,20},{1,17},{... | collective-permute-start | bytes 552968 | tf_op jit(solution)/shard_map/ppermute | solution.py:31
  12.8 0.0 collective-permute-done.10.refs_1_
  12.8 1.5 %collective-permute-start.5 = (bf16[80,1152]{1,0:T(8,128)(2,1)S(1)}, bf16[80,1152]{1,0:T(8,128)(2,1)S(1)}, u32[]{:S(2)}, u32[]{:S(2)}) collective-permute-start(bf16[80,1152]{1,0:T(8,128)(2,1)S(1)} %forward.1.small_ref.refs_0_.refs_4_), channel_id=1, source_target_pairs={{0,8},{4,20},{8,0},{12,28},{16,24},{20,4},{24,16},{28,12},{1,9},{5... | collective-permute-start | bytes 552968 | tf_op jit(solution)/shard_map/ppermute | solution.py:31
  14.3 0.0 collective-permute-done.12.refs_3_
  14.3 1.0 %collective-permute-start.6 = (bf16[80,1152]{1,0:T(8,128)(2,1)S(1)}, bf16[80,1152]{1,0:T(8,128)(2,1)S(1)}, u32[]{:S(2)}, u32[]{:S(2)}) collective-permute-start(bf16[80,1152]{1,0:T(8,128)(2,1)S(1)} %forward.1.small_ref.refs_0_.refs_4_), channel_id=1, source_target_pairs={{0,24},{4,28},{8,16},{12,20},{16,8},{20,12},{24,0},{28,4},{1,25},{... | collective-permute-start | bytes 552968 | tf_op jit(solution)/shard_map/ppermute | solution.py:31
  15.3 1.0 %collective-permute-done.13.refs_4_ = bf16[2,80,512]{2,1,0:T(8,128)(2,1)S(1)} collective-permute-done((bf16[2,80,512]{2,1,0:T(8,128)(2,1)S(1)}, bf16[2,80,512]{2,1,0:T(8,128)(2,1)S(1)}, u32[]{:S(2)}, u32[]{:S(2)}) %collective-permute-start.13) | collective-permute-done | bytes 163872 | tf_op jit(solution)/shard_map/ppermute | solution.py:31
  16.2 2.1 %collective-permute-done.11.refs_2_ = bf16[2,80,512]{2,1,0:T(8,128)(2,1)S(1)} collective-permute-done((bf16[2,80,512]{2,1,0:T(8,128)(2,1)S(1)}, bf16[2,80,512]{2,1,0:T(8,128)(2,1)S(1)}, u32[]{:S(2)}, u32[]{:S(2)}) %collective-permute-start.11) | collective-permute-done | bytes 163872 | tf_op jit(solution)/shard_map/ppermute | solution.py:31
  18.3 0.0 collective-permute-start.15
  18.3 2.6 %collective-permute-done.4.refs_2_.refs_6_ = bf16[80,1152]{1,0:T(8,128)(2,1)S(1)} collective-permute-done((bf16[80,1152]{1,0:T(8,128)(2,1)S(1)}, bf16[80,1152]{1,0:T(8,128)(2,1)S(1)}, u32[]{:S(2)}, u32[]{:S(2)}) %collective-permute-start.4) | collective-permute-done | bytes 184352 | tf_op jit(solution)/shard_map/ppermute | solution.py:31
  20.9 0.0 collective-permute-start.7
  20.9 0.0 collective-permute-done.5.refs_3_.refs_7_
  20.9 0.5 %collective-permute-start.16 = (bf16[2,80,512]{2,1,0:T(8,128)(2,1)S(1)}, bf16[2,80,512]{2,1,0:T(8,128)(2,1)S(1)}, u32[]{:S(2)}, u32[]{:S(2)}) collective-permute-start(bf16[2,80,512]{2,1,0:T(8,128)(2,1)S(1)} %collective-permute-done.13.refs_4_), channel_id=1, source_target_pairs={{0,4},{4,0},{8,12},{12,8},{16,20},{20,16},{24,28},{28,24},{1,5},{5... | collective-permute-start | bytes 491528 | tf_op jit(solution)/shard_map/ppermute | solution.py:21
  21.4 3.3 %collective-permute-done.6.refs_4_.refs_8_ = bf16[80,1152]{1,0:T(8,128)(2,1)S(1)} collective-permute-done((bf16[80,1152]{1,0:T(8,128)(2,1)S(1)}, bf16[80,1152]{1,0:T(8,128)(2,1)S(1)}, u32[]{:S(2)}, u32[]{:S(2)}) %collective-permute-start.6) | collective-permute-done | bytes 184352 | tf_op jit(solution)/shard_map/ppermute | solution.py:31
  24.7 0.1 collective-permute-start.14
  24.8 0.4 collective-permute-start.8
  25.2 0.0 collective-permute-done.15.refs_6_
  25.2 0.1 collective-permute-start.9
  25.4 1.2 %back.1 = (bf16[20,2048]{1,0:T(8,128)(2,1)S(1)}, bf16[20,2048]{1,0:T(8,128)(2,1)S(1)}, bf16[20,2048]{1,0:T(8,128)(2,1)S(1)}, bf16[20,2048]{1,0:T(8,128)(2,1)S(1)}) custom-call(bf16[80,1152]{1,0:T(8,128)(2,1)S(1)} %forward.1.small_ref.refs_0_.refs_4_, bf16[1,3,2048,384]{3,2,1,0:T(8,128)(2,1)S(1)} %copy-done), custom_call_target="tpu_custom_call" | custom-call | flops 251658240 | bytes 3145728 | tf_op jit(solution)/shard_map/back/pallas_call | solution.py:225
  26.5 0.6 %shard_map.78 = (f32[2,400,400]{2,1,0:T(8,128)S(1)}, bf16[2,256,400]{2,1,0:T(8,128)(2,1)S(1)}) custom-call(bf16[2,80,512]{2,1,0:T(8,128)(2,1)S(1)} %get-tuple-element.13.refs_0_, bf16[2,80,512]{2,1,0:T(8,128)(2,1)S(1)} %collective-permute-done.10.refs_1_, bf16[2,80,512]{2,1,0:T(8,128)(2,1)S(1)} %collective-permute-done.11.refs_2_, ...), custom_call_target="tpu_custom_call" | custom-call | flops 327680000 | bytes 2508800 | tf_op jit(solution)/shard_map/pallas_call | solution.py:300
  27.1 0.0 collective-permute-done.16.refs_7_
  27.2 1.6 %collective-permute-start = (bf16[20,2048]{1,0:T(8,128)(2,1)S(1)}, bf16[20,2048]{1,0:T(8,128)(2,1)S(1)}, u32[]{:S(2)}, u32[]{:S(2)}) collective-permute-start(bf16[20,2048]{1,0:T(8,128)(2,1)S(1)} %get-tuple-element.17), channel_id=1, source_target_pairs={{0,1},{1,0},{2,3},{3,2},{4,5},{5,4},{6,7},{7,6},{8,9},{9,8},{10,11... | collective-permute-start | bytes 245768 | tf_op jit(solution)/shard_map/ppermute | solution.py:21
  28.8 0.0 collective-permute-done.14.refs_5_
  28.8 2.6 %collective-permute-start.1 = (bf16[20,2048]{1,0:T(8,128)(2,1)S(1)}, bf16[20,2048]{1,0:T(8,128)(2,1)S(1)}, u32[]{:S(2)}, u32[]{:S(2)}) collective-permute-start(bf16[20,2048]{1,0:T(8,128)(2,1)S(1)} %get-tuple-element.18), channel_id=1, source_target_pairs={{0,2},{1,3},{2,0},{3,1},{4,6},{5,7},{6,4},{7,5},{8,10},{9,11},{10,... | collective-permute-start | bytes 245768 | tf_op jit(solution)/shard_map/ppermute | solution.py:21
  31.4 0.0 collective-permute-done.7.refs_5_.refs_9_
  31.4 0.2 collective-permute-start.2
  31.6 1.2 %first.1.refs_9_ = f32[24,128]{1,0:T(8,128)S(1)} custom-call(bf16[80,1152]{1,0:T(8,128)(2,1)S(1)} %forward.1.small_ref.refs_0_.refs_4_, bf16[80,1152]{1,0:T(8,128)(2,1)S(1)} %collective-permute-done.3.refs_1_.refs_5_, bf16[80,1152]{1,0:T(8,128)(2,1)S(1)} %collective-permute-done.4.refs_2_.refs_6_, ...), custom_call_target="tpu_custom_call" | custom-call | flops 471859200 | bytes 2621440 | tf_op jit(solution)/shard_map/first/pallas_call | solution.py:377
  32.8 0.6 %shard_map.77 = (f32[2,240,640]{2,1,0:T(8,128)S(1)}, bf16[2,256,240]{2,1,0:T(8,128)(2,1)S(1)}) custom-call(bf16[2,80,512]{2,1,0:T(8,128)(2,1)S(1)} %get-tuple-element.13.refs_0_, bf16[2,80,512]{2,1,0:T(8,128)(2,1)S(1)} %collective-permute-done.10.refs_1_, bf16[2,80,512]{2,1,0:T(8,128)(2,1)S(1)} %collective-permute-done.11.refs_2_, ...), custom_call_target="tpu_custom_call" | custom-call | flops 314572800 | bytes 3194880 | tf_op jit(solution)/shard_map/pallas_call | solution.py:300
  33.5 0.0 copy-start.4
  33.5 0.0 copy-start.1
  33.5 1.2 %last.1 = f32[24,128]{1,0:T(8,128)S(1)} custom-call(bf16[80,1152]{1,0:T(8,128)(2,1)S(1)} %forward.1.small_ref.refs_0_.refs_4_, bf16[80,1152]{1,0:T(8,128)(2,1)S(1)} %collective-permute-done.3.refs_1_.refs_5_, bf16[80,1152]{1,0:T(8,128)(2,1)S(1)} %collective-permute-done.4.refs_2_.refs_6_, bf16[80,1152]{1,0:T(8,128)(2,1)S(1)} %collective-permute-done.5.refs_3_.refs_7_, ...), custom_call_target="tpu_custom_call" | custom-call | flops 235929600 | bytes 2293760 | tf_op jit(solution)/shard_map/last/pallas_call | solution.py:390
  34.7 0.4 collective-permute-start.17
  35.0 3.4 %collective-permute-done.17 = f32[24,128]{1,0:T(8,128)S(1)} collective-permute-done((f32[24,128]{1,0:T(8,128)S(1)}, f32[24,128]{1,0:T(8,128)S(1)}, u32[]{:S(2)}, u32[]{:S(2)}) %collective-permute-start.17) | collective-permute-done | bytes 12320 | tf_op jit(solution)/shard_map/ppermute | solution.py:21
  38.4 1.5 %collective-permute-start.18 = (f32[24,128]{1,0:T(8,128)S(1)}, f32[24,128]{1,0:T(8,128)S(1)}, u32[]{:S(2)}, u32[]{:S(2)}) collective-permute-start(f32[24,128]{1,0:T(8,128)S(1)} %add.3.refs_0_), channel_id=1, source_target_pairs={{0,8},{4,12},{8,0},{12,4},{16,24},{20,28},{24,16},{28,20},{1,9},{5... | collective-permute-start | bytes 36872 | tf_op jit(solution)/shard_map/ppermute | solution.py:21
  39.9 0.9 %token_.1 = bf16[1,20,2048]{2,1,0:T(8,128)(2,1)} custom-call(s32[1,4,20]{2,1,0:T(4,128)S(1)} %bitcast.1, bf16[20,2048]{1,0:T(8,128)(2,1)S(1)} %get-tuple-element.16.refs_0_, bf16[20,2048]{1,0:T(8,128)(2,1)S(1)} %collective-permute-done.refs_1_, bf16[20,2048]{1,0:T(8,128)(2,1)S(1)} %collective-permute-done.1.refs_2_, ...), custom_call_target="tpu_custom_call" | custom-call | flops 10485760 | bytes 655360 | tf_op jit(solution)/shard_map/token/pallas_call | solution.py:264
  40.9 1.3 %collective-permute-done.18.refs_1_ = f32[24,128]{1,0:T(8,128)S(1)} collective-permute-done((f32[24,128]{1,0:T(8,128)S(1)}, f32[24,128]{1,0:T(8,128)S(1)}, u32[]{:S(2)}, u32[]{:S(2)}) %collective-permute-start.18) | collective-permute-done | bytes 12320 | tf_op jit(solution)/shard_map/ppermute | solution.py:21
  42.1 2.1 %final.1 = f32[1,3,256,384]{3,2,1,0:T(8,128)} custom-call(f32[24,128]{1,0:T(8,128)S(1)} %add.3.refs_0_, f32[24,128]{1,0:T(8,128)S(1)} %collective-permute-done.18.refs_1_, bf16[2,256,400]{2,1,0:T(8,128)(2,1)S(1)} %get-tuple-element.22.refs_2_, bf16[2,256,240]{2,1,0:T(8,128)(2,1)S(1)} %get-tuple-element.23.refs_3_, ...), custom_call_target="tpu_custom_call" | custom-call | flops 377487360 | bytes 3833856 | tf_op jit(solution)/shard_map/final/pallas_call | solution.py:455
  (13 shorter events, 0.0 us)
Async XLA Ops:
  0.6 1.0 %copy-start.2 = (bf16[1,128,2048]{2,1,0:T(8,128)(2,1)S(1)}, bf16[1,128,2048]{2,1,0:T(8,128)(2,1)}, u32[]{:S(2)}) copy-start(bf16[1,128,2048]{2,1,0:T(8,128)(2,1)} %x_hbm.1) | copy-start | bytes 1572868
  1.7 1.0 %copy-start.3 = (bf16[1,128,2048]{2,1,0:T(8,128)(2,1)S(1)}, bf16[1,128,2048]{2,1,0:T(8,128)(2,1)}, u32[]{:S(2)}) copy-start(bf16[1,128,2048]{2,1,0:T(8,128)(2,1)} %cot_hbm.1) | copy-start | bytes 1572868
  2.7 0.7 %copy-start.5 = (f32[1,128]{1,0:T(1,128)S(1)}, f32[1,128]{1,0:T(1,128)}, u32[]{:S(2)}) copy-start(f32[1,128]{1,0:T(1,128)} %gate_hbm.1) | copy-start | bytes 1540
  3.7 9.1 %collective-permute-start.10 = (bf16[2,80,512]{2,1,0:T(8,128)(2,1)S(1)}, bf16[2,80,512]{2,1,0:T(8,128)(2,1)S(1)}, u32[]{:S(2)}, u32[]{:S(2)}) collective-permute-start(bf16[2,80,512]{2,1,0:T(8,128)(2,1)S(1)} %get-tuple-element.13.refs_0_), channel_id=1, source_target_pairs={{0,4},{4,0},{8,12},{12,8},{16,20},{20,16},{24,28},{28,24},{1,5},{5... | collective-permute-start | bytes 491528 | tf_op jit(solution)/shard_map/ppermute | solution.py:21
  4.3 10.0 %collective-permute-start.12 = (bf16[2,80,512]{2,1,0:T(8,128)(2,1)S(1)}, bf16[2,80,512]{2,1,0:T(8,128)(2,1)S(1)}, u32[]{:S(2)}, u32[]{:S(2)}) collective-permute-start(bf16[2,80,512]{2,1,0:T(8,128)(2,1)S(1)} %get-tuple-element.14.refs_2_), channel_id=1, source_target_pairs={{0,8},{4,20},{8,0},{12,28},{16,24},{20,4},{24,16},{28,12},{1,9},{5... | collective-permute-start | bytes 491528 | tf_op jit(solution)/shard_map/ppermute | solution.py:31
  6.8 9.4 %collective-permute-start.13 = (bf16[2,80,512]{2,1,0:T(8,128)(2,1)S(1)}, bf16[2,80,512]{2,1,0:T(8,128)(2,1)S(1)}, u32[]{:S(2)}, u32[]{:S(2)}) collective-permute-start(bf16[2,80,512]{2,1,0:T(8,128)(2,1)S(1)} %get-tuple-element.15.refs_3_), channel_id=1, source_target_pairs={{0,24},{4,28},{8,16},{12,20},{16,8},{20,12},{24,0},{28,4},{1,25},{... | collective-permute-start | bytes 491528 | tf_op jit(solution)/shard_map/ppermute | solution.py:31
  8.3 2.5 %copy-start = (bf16[1,3,2048,384]{3,2,1,0:T(8,128)(2,1)S(1)}, bf16[1,3,2048,384]{3,2,1,0:T(8,128)(2,1)}, u32[]{:S(2)}) copy-start(bf16[1,3,2048,384]{3,2,1,0:T(8,128)(2,1)} %w_ref.1) | copy-start | bytes 14155780
  9.7 8.6 %collective-permute-start.11 = (bf16[2,80,512]{2,1,0:T(8,128)(2,1)S(1)}, bf16[2,80,512]{2,1,0:T(8,128)(2,1)S(1)}, u32[]{:S(2)}, u32[]{:S(2)}) collective-permute-start(bf16[2,80,512]{2,1,0:T(8,128)(2,1)S(1)} %pack_one.1.refs_1_), channel_id=1, source_target_pairs={{0,16},{4,12},{8,24},{12,4},{16,0},{20,28},{24,8},{28,20},{1,17},{... | collective-permute-start | bytes 491528 | tf_op jit(solution)/shard_map/ppermute | solution.py:31
  11.7 9.2 %collective-permute-start.4 = (bf16[80,1152]{1,0:T(8,128)(2,1)S(1)}, bf16[80,1152]{1,0:T(8,128)(2,1)S(1)}, u32[]{:S(2)}, u32[]{:S(2)}) collective-permute-start(bf16[80,1152]{1,0:T(8,128)(2,1)S(1)} %forward.1.small_ref.refs_0_.refs_4_), channel_id=1, source_target_pairs={{0,16},{4,12},{8,24},{12,4},{16,0},{20,28},{24,8},{28,20},{1,17},{... | collective-permute-start | bytes 552968 | tf_op jit(solution)/shard_map/ppermute | solution.py:31
  12.8 8.1 %collective-permute-start.5 = (bf16[80,1152]{1,0:T(8,128)(2,1)S(1)}, bf16[80,1152]{1,0:T(8,128)(2,1)S(1)}, u32[]{:S(2)}, u32[]{:S(2)}) collective-permute-start(bf16[80,1152]{1,0:T(8,128)(2,1)S(1)} %forward.1.small_ref.refs_0_.refs_4_), channel_id=1, source_target_pairs={{0,8},{4,20},{8,0},{12,28},{16,24},{20,4},{24,16},{28,12},{1,9},{5... | collective-permute-start | bytes 552968 | tf_op jit(solution)/shard_map/ppermute | solution.py:31
  14.3 10.4 %collective-permute-start.6 = (bf16[80,1152]{1,0:T(8,128)(2,1)S(1)}, bf16[80,1152]{1,0:T(8,128)(2,1)S(1)}, u32[]{:S(2)}, u32[]{:S(2)}) collective-permute-start(bf16[80,1152]{1,0:T(8,128)(2,1)S(1)} %forward.1.small_ref.refs_0_.refs_4_), channel_id=1, source_target_pairs={{0,24},{4,28},{8,16},{12,20},{16,8},{20,12},{24,0},{28,4},{1,25},{... | collective-permute-start | bytes 552968 | tf_op jit(solution)/shard_map/ppermute | solution.py:31
  16.2 8.6 %collective-permute-start.3 = (bf16[80,1152]{1,0:T(8,128)(2,1)S(1)}, bf16[80,1152]{1,0:T(8,128)(2,1)S(1)}, u32[]{:S(2)}, u32[]{:S(2)}) collective-permute-start(bf16[80,1152]{1,0:T(8,128)(2,1)S(1)} %forward.1.small_ref.refs_0_.refs_4_), channel_id=1, source_target_pairs={{0,4},{4,0},{8,12},{12,8},{16,20},{20,16},{24,28},{28,24},{1,5},{5... | collective-permute-start | bytes 552968 | tf_op jit(solution)/shard_map/ppermute | solution.py:21
  18.3 6.9 %collective-permute-start.15 = (bf16[2,80,512]{2,1,0:T(8,128)(2,1)S(1)}, bf16[2,80,512]{2,1,0:T(8,128)(2,1)S(1)}, u32[]{:S(2)}, u32[]{:S(2)}) collective-permute-start(bf16[2,80,512]{2,1,0:T(8,128)(2,1)S(1)} %collective-permute-done.12.refs_3_), channel_id=1, source_target_pairs={{0,4},{4,0},{8,12},{12,8},{16,20},{20,16},{24,28},{28,24},{1,5},{5... | collective-permute-start | bytes 491528 | tf_op jit(solution)/shard_map/ppermute | solution.py:21
  20.9 10.5 %collective-permute-start.7 = (bf16[80,1152]{1,0:T(8,128)(2,1)S(1)}, bf16[80,1152]{1,0:T(8,128)(2,1)S(1)}, u32[]{:S(2)}, u32[]{:S(2)}) collective-permute-start(bf16[80,1152]{1,0:T(8,128)(2,1)S(1)} %collective-permute-done.4.refs_2_.refs_6_), channel_id=1, source_target_pairs={{0,4},{4,0},{8,12},{12,8},{16,20},{20,16},{24,28},{28,24},{1,5},{5... | collective-permute-start | bytes 552968 | tf_op jit(solution)/shard_map/ppermute | solution.py:21
  20.9 6.3 %collective-permute-start.16 = (bf16[2,80,512]{2,1,0:T(8,128)(2,1)S(1)}, bf16[2,80,512]{2,1,0:T(8,128)(2,1)S(1)}, u32[]{:S(2)}, u32[]{:S(2)}) collective-permute-start(bf16[2,80,512]{2,1,0:T(8,128)(2,1)S(1)} %collective-permute-done.13.refs_4_), channel_id=1, source_target_pairs={{0,4},{4,0},{8,12},{12,8},{16,20},{20,16},{24,28},{28,24},{1,5},{5... | collective-permute-start | bytes 491528 | tf_op jit(solution)/shard_map/ppermute | solution.py:21
  24.7 4.1 %collective-permute-start.14 = (bf16[2,80,512]{2,1,0:T(8,128)(2,1)S(1)}, bf16[2,80,512]{2,1,0:T(8,128)(2,1)S(1)}, u32[]{:S(2)}, u32[]{:S(2)}) collective-permute-start(bf16[2,80,512]{2,1,0:T(8,128)(2,1)S(1)} %collective-permute-done.11.refs_2_), channel_id=1, source_target_pairs={{0,4},{4,0},{8,12},{12,8},{16,20},{20,16},{24,28},{28,24},{1,5},{5... | collective-permute-start | bytes 491528 | tf_op jit(solution)/shard_map/ppermute | solution.py:21
  24.8 8.6 %collective-permute-start.8 = (bf16[80,1152]{1,0:T(8,128)(2,1)S(1)}, bf16[80,1152]{1,0:T(8,128)(2,1)S(1)}, u32[]{:S(2)}, u32[]{:S(2)}) collective-permute-start(bf16[80,1152]{1,0:T(8,128)(2,1)S(1)} %collective-permute-done.5.refs_3_.refs_7_), channel_id=1, source_target_pairs={{0,4},{4,0},{8,12},{12,8},{16,20},{20,16},{24,28},{28,24},{1,5},{5... | collective-permute-start | bytes 552968 | tf_op jit(solution)/shard_map/ppermute | solution.py:21
  25.2 8.2 %collective-permute-start.9 = (bf16[80,1152]{1,0:T(8,128)(2,1)S(1)}, bf16[80,1152]{1,0:T(8,128)(2,1)S(1)}, u32[]{:S(2)}, u32[]{:S(2)}) collective-permute-start(bf16[80,1152]{1,0:T(8,128)(2,1)S(1)} %collective-permute-done.6.refs_4_.refs_8_), channel_id=1, source_target_pairs={{0,4},{4,0},{8,12},{12,8},{16,20},{20,16},{24,28},{28,24},{1,5},{5... | collective-permute-start | bytes 552968 | tf_op jit(solution)/shard_map/ppermute | solution.py:21
  27.2 12.8 %collective-permute-start = (bf16[20,2048]{1,0:T(8,128)(2,1)S(1)}, bf16[20,2048]{1,0:T(8,128)(2,1)S(1)}, u32[]{:S(2)}, u32[]{:S(2)}) collective-permute-start(bf16[20,2048]{1,0:T(8,128)(2,1)S(1)} %get-tuple-element.17), channel_id=1, source_target_pairs={{0,1},{1,0},{2,3},{3,2},{4,5},{5,4},{6,7},{7,6},{8,9},{9,8},{10,11... | collective-permute-start | bytes 245768 | tf_op jit(solution)/shard_map/ppermute | solution.py:21
  28.8 11.1 %collective-permute-start.1 = (bf16[20,2048]{1,0:T(8,128)(2,1)S(1)}, bf16[20,2048]{1,0:T(8,128)(2,1)S(1)}, u32[]{:S(2)}, u32[]{:S(2)}) collective-permute-start(bf16[20,2048]{1,0:T(8,128)(2,1)S(1)} %get-tuple-element.18), channel_id=1, source_target_pairs={{0,2},{1,3},{2,0},{3,1},{4,6},{5,7},{6,4},{7,5},{8,10},{9,11},{10,... | collective-permute-start | bytes 245768 | tf_op jit(solution)/shard_map/ppermute | solution.py:21
  31.4 8.6 %collective-permute-start.2 = (bf16[20,2048]{1,0:T(8,128)(2,1)S(1)}, bf16[20,2048]{1,0:T(8,128)(2,1)S(1)}, u32[]{:S(2)}, u32[]{:S(2)}) collective-permute-start(bf16[20,2048]{1,0:T(8,128)(2,1)S(1)} %get-tuple-element.19), channel_id=1, source_target_pairs={{0,3},{1,2},{2,1},{3,0},{4,7},{5,6},{6,5},{7,4},{8,11},{9,10},{10,... | collective-permute-start | bytes 245768 | tf_op jit(solution)/shard_map/ppermute | solution.py:21
  33.5 6.5 %copy-start.4 = (s32[1,20,4]{1,2,0:T(4,128)S(1)}, s32[1,20,4]{1,2,0:T(4,128)}, u32[]{:S(2)}) copy-start(s32[1,20,4]{1,2,0:T(4,128)} %param.9) | copy-start | bytes 964
  33.5 8.7 %copy-start.1 = (f32[1,3,256,384]{3,2,1,0:T(8,128)S(1)}, f32[1,3,256,384]{3,2,1,0:T(8,128)}, u32[]{:S(2)}) copy-start(f32[1,3,256,384]{3,2,1,0:T(8,128)} %refs_12_.1) | copy-start | bytes 3538948
  34.7 3.8 %collective-permute-start.17 = (f32[24,128]{1,0:T(8,128)S(1)}, f32[24,128]{1,0:T(8,128)S(1)}, u32[]{:S(2)}, u32[]{:S(2)}) collective-permute-start(f32[24,128]{1,0:T(8,128)S(1)} %last.1), channel_id=1, source_target_pairs={{0,16},{4,20},{8,24},{12,28},{16,0},{20,4},{24,8},{28,12},{1,17},{... | collective-permute-start | bytes 36872 | tf_op jit(solution)/shard_map/ppermute | solution.py:21
  38.4 3.7 %collective-permute-start.18 = (f32[24,128]{1,0:T(8,128)S(1)}, f32[24,128]{1,0:T(8,128)S(1)}, u32[]{:S(2)}, u32[]{:S(2)}) collective-permute-start(f32[24,128]{1,0:T(8,128)S(1)} %add.3.refs_0_), channel_id=1, source_target_pairs={{0,8},{4,12},{8,0},{12,4},{16,24},{20,28},{24,16},{28,20},{1,9},{5... | collective-permute-start | bytes 36872 | tf_op jit(solution)/shard_map/ppermute | solution.py:21
